TPU v7x, 32 devices: a whole 2x2x4 slice. The times are simulated.
32 devices in a mesh: mode: 8 (over z, x), space: 4 (over y, core).
Axes of the slice: x: 2, y: 2, z: 4, core: 2. Of those that a mesh axis runs over, the one named last changes fastest.
Arguments:
- forcing: float32 [64, 64, 256], P('mode', 'space'), may hold values from -8 to 8
- mean_field: float32 [64, 256], P('space'), may hold values from 0.5 to 2
- coef_fields: float32 [28, 64, 256], P(None, 'space'), may hold values from -3 to 3
- color: int32 [64], replicated, may hold values from 0 to 3, as said below
- pair_src: int32 [4, 64, 24], P(None, 'mode'), may hold values from 0 to 63, as said below
- pair_field: int32 [4, 64, 24], P(None, 'mode'), may hold values from 0 to 27
- pair_value: float32 [4, 64, 24], P(None, 'mode'), may hold values from -1.25 to 1.25
Outputs:
- solution: float32 [64, 64, 256], P('mode', 'space')
- residual: float32 [64, 64, 256], P('mode', 'space')
Inputs may be any that keep to these rules, and one draw needn't show every extreme that they name: `color`: every aligned block of 8 modes holds exactly 2 modes of each batch. `pair_src`: the entries of batch c name only modes whose color is c.
All inputs are finite; a program needn't handle non-finite values.
Results may differ from a plain program's by a relative error of at most 0.0001.
Values sent between devices are 32-bit elements; how exact they have to be, the bound alone decides.
A program may use at most 64 MiB of HBM per device.

v0:
```python
import jax
import jax.numpy as jnp
from jax import lax
from jax.sharding import PartitionSpec as P

SWEEPS = 2


def with_halo(block, sides, width):
    for axis, dim in sides:
        count = lax.axis_size(axis)
        forward = [(i, i + 1) for i in range(count - 1)]
        backward = [(target, source) for source, target in forward]
        low = lax.ppermute(
            lax.slice_in_dim(block, block.shape[dim] - width, None, axis=dim), axis, forward
        )
        high = lax.ppermute(lax.slice_in_dim(block, 0, width, axis=dim), axis, backward)
        block = jnp.concatenate([low, block, high], axis=dim)
    return block


def stencil_ext(coeff_ext, value_ext):
    coeff_mid = coeff_ext[1:-1]
    value_mid = value_ext[1:-1]
    coeff_side = jnp.pad(coeff_mid, ((0, 0), (1, 1)))
    value_side = jnp.pad(value_mid, ((0, 0), (1, 1)))
    result = 0.5 * (coeff_mid + coeff_ext[2:]) * (value_mid - value_ext[2:])
    result = result + 0.5 * (coeff_mid + coeff_ext[:-2]) * (value_mid - value_ext[:-2])
    result = result + 0.5 * (coeff_mid + coeff_side[:, 2:]) * (value_mid - value_side[:, 2:])
    result = result + 0.5 * (coeff_mid + coeff_side[:, :-2]) * (value_mid - value_side[:, :-2])
    return result


def face_sum_ext(coeff_ext):
    coeff_mid = coeff_ext[1:-1]
    coeff_side = jnp.pad(coeff_mid, ((0, 0), (1, 1)))
    result = 0.5 * (coeff_mid + coeff_ext[2:])
    result = result + 0.5 * (coeff_mid + coeff_ext[:-2])
    result = result + 0.5 * (coeff_mid + coeff_side[:, 2:])
    result = result + 0.5 * (coeff_mid + coeff_side[:, :-2])
    return result


def couple(gathered, sources, field_ids, weights, stacked_ext):

    def reader(reader_entry):
        source_rows, field_rows, weight_rows = reader_entry
        values = jnp.take(gathered, source_rows, axis=0)
        coeffs = jnp.take(stacked_ext, field_rows + 1, axis=0)
        fluxes = jax.vmap(stencil_ext)(coeffs, values)
        return jnp.sum(weight_rows[:, None, None] * fluxes, axis=0)

    return lax.map(reader, (sources, field_ids, weights))


def on_device(forcing, mean_field, coef_fields, color, pair_src, pair_field, pair_value):
    mode_dev = forcing.shape[0]
    batches = pair_src.shape[0]
    per_batch = mode_dev // batches
    stacked = jnp.concatenate([mean_field[None], coef_fields], axis=0)
    stacked_ext = with_halo(stacked, (("space", 1),), 1)
    diag_sum = face_sum_ext(stacked_ext[0])
    grouped = color.reshape(-1, mode_dev)
    onehot = (grouped[:, :, None] == jnp.arange(batches, dtype=jnp.int32)[None, None, :]).astype(
        jnp.int32
    )
    earlier = jnp.cumsum(onehot, axis=1) - onehot
    ranking = jnp.sum(onehot * earlier, axis=2).reshape(-1)
    owners = jnp.arange(color.shape[0], dtype=jnp.int32) // mode_dev
    pool_rows = owners * per_batch + ranking
    source_rows = jnp.take(pool_rows, pair_src, axis=0)
    offset = lax.axis_index("mode") * mode_dev
    local_color = lax.dynamic_slice_in_dim(color, offset, mode_dev)
    local_rank = lax.dynamic_slice_in_dim(ranking, offset, mode_dev)
    positions = jnp.arange(mode_dev, dtype=jnp.int32)
    slot_numbers = jnp.arange(per_batch, dtype=jnp.int32)
    solution = jnp.zeros(forcing.shape, jnp.float32)
    coupled = jnp.zeros(forcing.shape, jnp.float32)
    for sweep_idx in range(SWEEPS):
        for color_idx in range(batches):
            active = local_color == color_idx
            update = jnp.where(active[:, None, None], (forcing - coupled) / diag_sum, 0.0)
            solution = solution + update
            selected = (active[None, :] & (local_rank[None, :] == slot_numbers[:, None])).astype(
                jnp.int32
            )
            chosen = jnp.sum(positions[None, :] * selected, axis=1)
            own_update = jnp.take(update, chosen, axis=0)
            inner = lax.all_gather(own_update, "mode", axis=0, tiled=True)
            gathered = with_halo(inner, (("space", 1),), 1)
            coupled = coupled + couple(
                gathered,
                source_rows[color_idx],
                pair_field[color_idx],
                pair_value[color_idx],
                stacked_ext,
            )
    return (solution, forcing - coupled)


def solution(mesh):
    return jax.shard_map(
        on_device,
        mesh=mesh,
        in_specs=(
            P("mode", "space", None),
            P("space", None),
            P(None, "space", None),
            P(),
            P(None, "mode", None),
            P(None, "mode", None),
            P(None, "mode", None),
        ),
        out_specs=(P("mode", "space", None), P("mode", "space", None)),
        check_vma=False,
    )
```

profile of v0, /device:TPU:0, one launch (start us, length us, event | category | flops | bytes accessed | tf_op | source)
XLA Modules:
  0.0 513.9 jit_solution(9934791065722571374)
XLA Ops:
  0.6 1.1 pad_maximum_fusion.10
  1.7 1.3 collective-permute-start
  3.0 3.0 collective-permute-start.1
  9.2 4.8 gather_fusion.16
  15.7 0.8 copy-done
  17.2 32.6 %all_gather.24 = f32[16,16,256]{2,1,0:T(8,128)S(1)} all-gather(f32[2,16,256]{2,1,0:T(8,128)S(1)} %broadcast_select_fusion.23), channel_id=1, replica_groups=mesh['mode'=8,'space'=4] {'mode'}, dimensions={0}, use_global_device_ids=true | all-gather | bytes 294912 | tf_op jit(solution)/shard_map/all_gather | solution.py:89
  49.7 1.3 collective-permute-start.2
  51.0 1.3 collective-permute-start.3
  52.5 3.4 collective-permute-done.3
  56.0 17.8 %while.96 = (s32[]{:T(128)}, f32[8,16,256]{2,1,0:T(8,128)S(1)}, f32[8,24]{1,0:T(8,128)S(1)}, s32[8,24]{1,0:T(8,128)S(1)}, f32[29,18,256]{2,1,0:T(8,128)S(1)}, /*...) while((s32[]{:T(128)}, f32[8,16,256]{2,1,0:T(8,128)S(1)}, f32[8,24]{1,0:T(8,128)S(1)}, ...), condition=%wide.region_5.9_spmd, body=%wide.region_3.8_spmd.sunk | while | flops 2283834 | bytes 7529697 | solution.py:53
  75.0 30.7 %all_gather.25 = f32[16,16,256]{2,1,0:T(8,128)S(1)} all-gather(f32[2,16,256]{2,1,0:T(8,128)S(1)} %broadcast_select_fusion.22), channel_id=1, replica_groups=mesh['mode'=8,'space'=4] {'mode'}, dimensions={0}, use_global_device_ids=true | all-gather | bytes 294912 | tf_op jit(solution)/shard_map/all_gather | solution.py:89
  105.7 1.3 collective-permute-start.4
  107.0 1.3 collective-permute-start.5
  108.4 4.4 collective-permute-done.5
  112.9 17.8 %while.97 = (s32[]{:T(128)}, f32[8,16,256]{2,1,0:T(8,128)S(1)}, f32[8,24]{1,0:T(8,128)S(1)}, s32[8,24]{1,0:T(8,128)S(1)}, f32[29,18,256]{2,1,0:T(8,128)S(1)}, /*...) while((s32[]{:T(128)}, f32[8,16,256]{2,1,0:T(8,128)S(1)}, f32[8,24]{1,0:T(8,128)S(1)}, ...), condition=%wide.region_9.13_spmd, body=%wide.region_7.12_spmd.sunk | while | flops 2283834 | bytes 7529697 | solution.py:53
  131.9 30.7 %all_gather.26 = f32[16,16,256]{2,1,0:T(8,128)S(1)} all-gather(f32[2,16,256]{2,1,0:T(8,128)S(1)} %broadcast_select_fusion.21), channel_id=1, replica_groups=mesh['mode'=8,'space'=4] {'mode'}, dimensions={0}, use_global_device_ids=true | all-gather | bytes 294912 | tf_op jit(solution)/shard_map/all_gather | solution.py:89
  162.7 1.3 collective-permute-start.6
  164.0 1.3 collective-permute-start.7
  165.3 4.4 collective-permute-done.7
  169.8 17.8 %while.98 = (s32[]{:T(128)}, f32[8,16,256]{2,1,0:T(8,128)S(1)}, f32[8,24]{1,0:T(8,128)S(1)}, s32[8,24]{1,0:T(8,128)S(1)}, f32[29,18,256]{2,1,0:T(8,128)S(1)}, /*...) while((s32[]{:T(128)}, f32[8,16,256]{2,1,0:T(8,128)S(1)}, f32[8,24]{1,0:T(8,128)S(1)}, ...), condition=%wide.region_13.17_spmd, body=%wide.region_11.16_spmd.sunk | while | flops 2283834 | bytes 7529697 | solution.py:53
  188.9 30.7 %all_gather.27 = f32[16,16,256]{2,1,0:T(8,128)S(1)} all-gather(f32[2,16,256]{2,1,0:T(8,128)S(1)} %broadcast_select_fusion.20), channel_id=1, replica_groups=mesh['mode'=8,'space'=4] {'mode'}, dimensions={0}, use_global_device_ids=true | all-gather | bytes 294912 | tf_op jit(solution)/shard_map/all_gather | solution.py:89
  219.7 1.3 collective-permute-start.8
  221.0 1.3 collective-permute-start.9
  222.3 4.4 collective-permute-done.9
  226.8 23.1 %while.99 = (s32[]{:T(128)}, f32[8,16,256]{2,1,0:T(8,128)S(1)}, f32[8,24]{1,0:T(8,128)}, s32[8,24]{1,0:T(8,128)S(1)}, f32[29,18,256]{2,1,0:T(8,128)S(1)}, /*inde...) while((s32[]{:T(128)}, f32[8,16,256]{2,1,0:T(8,128)S(1)}, f32[8,24]{1,0:T(8,128)}, ...), condition=%wide.region_17.21_spmd, body=%wide.region_15.20_spmd.sunk | while | flops 2283834 | bytes 7529697 | solution.py:53
  251.4 30.7 %all_gather.28 = f32[16,16,256]{2,1,0:T(8,128)S(1)} all-gather(f32[2,16,256]{2,1,0:T(8,128)S(1)} %broadcast_select_fusion.19), channel_id=1, replica_groups=mesh['mode'=8,'space'=4] {'mode'}, dimensions={0}, use_global_device_ids=true | all-gather | bytes 294912 | tf_op jit(solution)/shard_map/all_gather | solution.py:89
  282.1 1.3 collective-permute-start.10
  283.4 1.3 collective-permute-start.11
  284.7 4.4 collective-permute-done.11
  289.2 23.2 %while.100 = (s32[]{:T(128)}, f32[8,16,256]{2,1,0:T(8,128)S(1)}, f32[8,24]{1,0:T(8,128)}, s32[8,24]{1,0:T(8,128)S(1)}, f32[29,18,256]{2,1,0:T(8,128)S(1)}, /*ind...) while((s32[]{:T(128)}, f32[8,16,256]{2,1,0:T(8,128)S(1)}, f32[8,24]{1,0:T(8,128)}, ...), condition=%wide.region_20.24_spmd, body=%wide.region_18.23_spmd.sunk | while | flops 2283834 | bytes 7529697 | solution.py:53
  312.5 1.6 divide_select_fusion.2
  314.7 30.7 %all_gather.29 = f32[16,16,256]{2,1,0:T(8,128)S(1)} all-gather(f32[2,16,256]{2,1,0:T(8,128)S(1)} %broadcast_select_fusion.18), channel_id=1, replica_groups=mesh['mode'=8,'space'=4] {'mode'}, dimensions={0}, use_global_device_ids=true | all-gather | bytes 294912 | tf_op jit(solution)/shard_map/all_gather | solution.py:89
  345.5 1.3 collective-permute-start.12
  346.8 1.3 collective-permute-start.13
  348.1 4.4 collective-permute-done.13
  353.3 27.8 %while.101 = (s32[]{:T(128)}, f32[8,16,256]{2,1,0:T(8,128)}, f32[8,24]{1,0:T(8,128)}, s32[8,24]{1,0:T(8,128)S(1)}, f32[29,18,256]{2,1,0:T(8,128)S(1)}, /*index=5...) while((s32[]{:T(128)}, f32[8,16,256]{2,1,0:T(8,128)}, f32[8,24]{1,0:T(8,128)}, ...), condition=%wide.region_23.27_spmd, body=%wide.region_21.26_spmd.sunk | while | flops 2283834 | bytes 7530205 | solution.py:53
  381.1 1.6 divide_select_fusion.1
  383.4 30.7 %all_gather.30 = f32[16,16,256]{2,1,0:T(8,128)S(1)} all-gather(f32[2,16,256]{2,1,0:T(8,128)S(1)} %broadcast_select_fusion.17), channel_id=1, replica_groups=mesh['mode'=8,'space'=4] {'mode'}, dimensions={0}, use_global_device_ids=true | all-gather | bytes 294912 | tf_op jit(solution)/shard_map/all_gather | solution.py:89
  414.2 1.3 collective-permute-start.14
  415.5 1.3 collective-permute-start.15
  416.8 4.4 collective-permute-done.15
  421.9 27.8 %while.102 = (s32[]{:T(128)}, f32[8,16,256]{2,1,0:T(8,128)}, f32[8,24]{1,0:T(8,128)}, s32[8,24]{1,0:T(8,128)S(1)}, f32[29,18,256]{2,1,0:T(8,128)S(1)}, /*index=5...) while((s32[]{:T(128)}, f32[8,16,256]{2,1,0:T(8,128)}, f32[8,24]{1,0:T(8,128)}, ...), condition=%wide.region_26.30_spmd, body=%wide.region_24.29_spmd.sunk | while | flops 2283834 | bytes 7530205 | solution.py:53
  449.7 1.8 add_add_fusion
  452.2 30.7 %all_gather.31 = f32[16,16,256]{2,1,0:T(8,128)S(1)} all-gather(f32[2,16,256]{2,1,0:T(8,128)S(1)} %broadcast_select_fusion.16), channel_id=1, replica_groups=mesh['mode'=8,'space'=4] {'mode'}, dimensions={0}, use_global_device_ids=true | all-gather | bytes 294912 | tf_op jit(solution)/shard_map/all_gather | solution.py:89
  482.9 1.3 collective-permute-start.16
  484.2 1.3 collective-permute-start.17
  485.5 4.4 collective-permute-done.17
  490.1 23.1 %while.103 = (s32[]{:T(128)}, f32[8,16,256]{2,1,0:T(8,128)S(1)}, f32[8,24]{1,0:T(8,128)}, s32[8,24]{1,0:T(8,128)S(1)}, f32[29,18,256]{2,1,0:T(8,128)S(1)}, /*ind...) while((s32[]{:T(128)}, f32[8,16,256]{2,1,0:T(8,128)S(1)}, f32[8,24]{1,0:T(8,128)}, ...), condition=%wide.region_29.33_spmd, body=%wide.region_27.32_spmd.sunk | while | flops 2283834 | bytes 7529697 | solution.py:53
  (896 shorter events, 187.8 us)
Async XLA Ops:
  1.7 13.8 %collective-permute-start = (f32[29,1,256]{2,1,0:T(1,128)S(1)}, f32[29,1,256]{2,1,0:T(1,128)S(1)}, u32[]{:S(2)}, u32[]{:S(2)}) collective-permute-start(f32[29,1,256]{2,1,0:T(1,128)S(1)} %get-tuple-element.904), channel_id=1, source_target_pairs={{1,0},{2,1},{3,2},{5,4},{6,5},{7,6},{9,8},{10,9},{11,10},{13,12},{... | collective-permute-start | bytes 89096 | tf_op jit(solution)/shard_map/ppermute | solution.py:17
  3.0 12.5 %collective-permute-start.1 = (f32[29,1,256]{2,1,0:T(1,128)S(1)}, f32[29,1,256]{2,1,0:T(1,128)S(1)}, u32[]{:S(2)}, u32[]{:S(2)}) collective-permute-start(f32[29,1,256]{2,1,0:T(1,128)S(1)} %get-tuple-element.905), channel_id=1, source_target_pairs={{0,1},{1,2},{2,3},{4,5},{5,6},{6,7},{8,9},{9,10},{10,11},{12,13},{... | collective-permute-start | bytes 89096 | tf_op jit(solution)/shard_map/ppermute | solution.py:14
  6.1 0.7 copy-start.19
  7.7 1.3 copy-start.5
  7.9 9.2 %copy-start.17 = (pred[2]{0:T(512)(128)(4,1)}, pred[2]{0:T(512)(128)(4,1)S(1)}, u32[]{:S(2)}) copy-start(pred[2]{0:T(512)(128)(4,1)S(1)} %compare_and_fusion.19) | copy-start | bytes 10
  7.9 67.0 %copy-start.15 = (pred[2]{0:T(512)(128)(4,1)}, pred[2]{0:T(512)(128)(4,1)S(1)}, u32[]{:S(2)}) copy-start(pred[2]{0:T(512)(128)(4,1)S(1)} %compare_and_fusion.18) | copy-start | bytes 10
  8.0 123.8 %copy-start.13 = (pred[2]{0:T(512)(128)(4,1)}, pred[2]{0:T(512)(128)(4,1)S(1)}, u32[]{:S(2)}) copy-start(pred[2]{0:T(512)(128)(4,1)S(1)} %compare_and_fusion.17) | copy-start | bytes 10
  9.2 6.4 %copy-start.1 = (f32[28,16,256]{2,1,0:T(8,128)S(1)}, f32[28,16,256]{2,1,0:T(8,128)}, u32[]{:S(2)}) copy-start(f32[28,16,256]{2,1,0:T(8,128)} %param.31) | copy-start | bytes 1376260
  9.2 6.4 %copy-start.4 = (f32[16,256]{1,0:T(8,128)S(1)}, f32[16,256]{1,0:T(8,128)}, u32[]{:S(2)}) copy-start(f32[16,256]{1,0:T(8,128)} %param.30) | copy-start | bytes 49156
  14.1 0.7 copy-start.6
  14.8 0.7 copy-start.7
  15.5 0.9 copy-start
  49.7 2.7 collective-permute-start.2
  51.0 4.8 collective-permute-start.3
  73.7 0.6 copy-start.10
  105.7 2.6 collective-permute-start.4
  107.0 5.7 %collective-permute-start.5 = (f32[16,1,256]{2,1,0:T(1,128)S(1)}, f32[16,1,256]{2,1,0:T(1,128)S(1)}, u32[]{:S(2)}, u32[]{:S(2)}) collective-permute-start(f32[16,1,256]{2,1,0:T(1,128)S(1)} %get-tuple-element.919), channel_id=1, source_target_pairs={{1,0},{2,1},{3,2},{5,4},{6,5},{7,6},{9,8},{10,9},{11,10},{13,12},{... | collective-permute-start | bytes 49160 | tf_op jit(solution)/shard_map/ppermute | solution.py:17
  130.7 0.6 copy-start.9
  162.6 2.6 copy-start.20
  162.7 2.6 collective-permute-start.6
  164.0 5.7 %collective-permute-start.7 = (f32[16,1,256]{2,1,0:T(1,128)S(1)}, f32[16,1,256]{2,1,0:T(1,128)S(1)}, u32[]{:S(2)}, u32[]{:S(2)}) collective-permute-start(f32[16,1,256]{2,1,0:T(1,128)S(1)} %get-tuple-element.917), channel_id=1, source_target_pairs={{1,0},{2,1},{3,2},{5,4},{6,5},{7,6},{9,8},{10,9},{11,10},{13,12},{... | collective-permute-start | bytes 49160 | tf_op jit(solution)/shard_map/ppermute | solution.py:17
  187.6 0.7 copy-start.8
  188.3 0.6 copy-start.11
  219.7 2.6 collective-permute-start.8
  221.0 5.7 %collective-permute-start.9 = (f32[16,1,256]{2,1,0:T(1,128)S(1)}, f32[16,1,256]{2,1,0:T(1,128)S(1)}, u32[]{:S(2)}, u32[]{:S(2)}) collective-permute-start(f32[16,1,256]{2,1,0:T(1,128)S(1)} %get-tuple-element.915), channel_id=1, source_target_pairs={{1,0},{2,1},{3,2},{5,4},{6,5},{7,6},{9,8},{10,9},{11,10},{13,12},{... | collective-permute-start | bytes 49160 | tf_op jit(solution)/shard_map/ppermute | solution.py:17
  226.8 23.1 %copy-start.3 = (f32[8,16,256]{2,1,0:T(8,128)S(1)}, f32[8,16,256]{2,1,0:T(8,128)}, u32[]{:S(2)}) copy-start(f32[8,16,256]{2,1,0:T(8,128)} %get-tuple-element.883) | copy-start | bytes 393220
  250.6 0.7 copy-start.18
  282.1 2.6 collective-permute-start.10
  283.4 5.7 %collective-permute-start.11 = (f32[16,1,256]{2,1,0:T(1,128)S(1)}, f32[16,1,256]{2,1,0:T(1,128)S(1)}, u32[]{:S(2)}, u32[]{:S(2)}) collective-permute-start(f32[16,1,256]{2,1,0:T(1,128)S(1)} %get-tuple-element.913), channel_id=1, source_target_pairs={{1,0},{2,1},{3,2},{5,4},{6,5},{7,6},{9,8},{10,9},{11,10},{13,12},{... | collective-permute-start | bytes 49160 | tf_op jit(solution)/shard_map/ppermute | solution.py:17
  314.1 0.6 copy-start.16
  345.5 2.6 collective-permute-start.12
  346.8 5.7 %collective-permute-start.13 = (f32[16,1,256]{2,1,0:T(1,128)S(1)}, f32[16,1,256]{2,1,0:T(1,128)S(1)}, u32[]{:S(2)}, u32[]{:S(2)}) collective-permute-start(f32[16,1,256]{2,1,0:T(1,128)S(1)} %get-tuple-element.911), channel_id=1, source_target_pairs={{1,0},{2,1},{3,2},{5,4},{6,5},{7,6},{9,8},{10,9},{11,10},{13,12},{... | collective-permute-start | bytes 49160 | tf_op jit(solution)/shard_map/ppermute | solution.py:17
  382.7 34.1 %copy-start.2 = (f32[8,16,256]{2,1,0:T(8,128)}, f32[8,16,256]{2,1,0:T(8,128)S(1)}, u32[]{:S(2)}) copy-start(f32[8,16,256]{2,1,0:T(8,128)S(1)} %get-tuple-element.876) | copy-start | bytes 393220
  382.7 0.6 copy-start.14
  414.2 2.6 collective-permute-start.14
  415.5 5.7 %collective-permute-start.15 = (f32[16,1,256]{2,1,0:T(1,128)S(1)}, f32[16,1,256]{2,1,0:T(1,128)S(1)}, u32[]{:S(2)}, u32[]{:S(2)}) collective-permute-start(f32[16,1,256]{2,1,0:T(1,128)S(1)} %get-tuple-element.909), channel_id=1, source_target_pairs={{1,0},{2,1},{3,2},{5,4},{6,5},{7,6},{9,8},{10,9},{11,10},{13,12},{... | collective-permute-start | bytes 49160 | tf_op jit(solution)/shard_map/ppermute | solution.py:17
  451.5 0.6 copy-start.12
  482.9 2.6 collective-permute-start.16
  484.2 5.7 %collective-permute-start.17 = (f32[16,1,256]{2,1,0:T(1,128)S(1)}, f32[16,1,256]{2,1,0:T(1,128)S(1)}, u32[]{:S(2)}, u32[]{:S(2)}) collective-permute-start(f32[16,1,256]{2,1,0:T(1,128)S(1)} %get-tuple-element.907), channel_id=1, source_target_pairs={{1,0},{2,1},{3,2},{5,4},{6,5},{7,6},{9,8},{10,9},{11,10},{13,12},{... | collective-permute-start | bytes 49160 | tf_op jit(solution)/shard_map/ppermute | solution.py:17
where the time goes:
time: 518 us; the launch traced here: 514 us
  blocking collectives  248 us (48%)
  local copies, waits for them, and re-layouts  134 us (26%)
  other arithmetic  65.5 us (13%)
  waiting for transfers between devices  34.5 us (7%)
  starting transfers between devices  25 us (5%)
  loops' own time  5.91 us (1%)
    all_gather x8, blocking collectives, on_device(): inner = lax.all_gather(own_update, 'mode', axis=0, tiled=True)  248 us
    reduce_sum x64, other arithmetic, reader(): return jnp.sum(weight_rows[:, None, None] * fluxes, axis=0)  38.6 us
    gather x64, local copies, waits for them, and re-layouts, reader(): values = jnp.take(gathered, source_rows, axis=0)  37.6 us
    gather x64, local copies, waits for them, and re-layouts, reader(): coeffs = jnp.take(stacked_ext, field_rows + 1, axis=0)  37.6 us
    ppermute x9, waiting for transfers between devices, with_halo(): lax.ppermute(lax.slice_in_dim(block, 0, width, axis=dim), axis, backward)  34.4 us
    mul x64, local copies, waits for them, and re-layouts, reader(): return jnp.sum(weight_rows[:, None, None] * fluxes, axis=0)  27.8 us
    ppermute x9, starting transfers between devices, with_halo(): lax.ppermute(lax.slice_in_dim(block, block.shape[dim] - width, None, axis...  13.4 us
    ppermute x9, starting transfers between devices, with_halo(): lax.ppermute(lax.slice_in_dim(block, 0, width, axis=dim), axis, backward)  11.6 us
  transfers between devices with their start and end apart: 18, of which 8 were waited for; matrix products, arithmetic and copies ran while one was open for 2% of the time, Pallas kernels for 0%

commit v1 on v0

--- a/solution.py
+++ b/solution.py
@@ -1,9 +1,16 @@
+import functools
+import math
+
 import jax
 import jax.numpy as jnp
 from jax import lax
+from jax.experimental import pallas as pl
+from jax.experimental.pallas import tpu as pltpu
 from jax.sharding import PartitionSpec as P
 
 SWEEPS = 2
+LANES = 128
+VMEM_BYTES = 67_000_000
 
 
 def with_halo(block, sides, width):
@@ -53,19 +60,23 @@
     return lax.map(reader, (sources, field_ids, weights))
 
 
-def on_device(forcing, mean_field, coef_fields, color, pair_src, pair_field, pair_value):
+def ranks(color, mode_dev, batches):
+    grouped = color.reshape(-1, mode_dev)
+    onehot = (grouped[:, :, None] == jnp.arange(batches, dtype=jnp.int32)[None, None, :]).astype(
+        jnp.int32
+    )
+    earlier = jnp.cumsum(onehot, axis=1) - onehot
+    return jnp.sum(onehot * earlier, axis=2).reshape(-1)
+
+
+def by_batch(forcing, mean_field, coef_fields, color, pair_src, pair_field, pair_value):
     mode_dev = forcing.shape[0]
     batches = pair_src.shape[0]
     per_batch = mode_dev // batches
     stacked = jnp.concatenate([mean_field[None], coef_fields], axis=0)
     stacked_ext = with_halo(stacked, (("space", 1),), 1)
     diag_sum = face_sum_ext(stacked_ext[0])
-    grouped = color.reshape(-1, mode_dev)
-    onehot = (grouped[:, :, None] == jnp.arange(batches, dtype=jnp.int32)[None, None, :]).astype(
-        jnp.int32
-    )
-    earlier = jnp.cumsum(onehot, axis=1) - onehot
-    ranking = jnp.sum(onehot * earlier, axis=2).reshape(-1)
+    ranking = ranks(color, mode_dev, batches)
     owners = jnp.arange(color.shape[0], dtype=jnp.int32) // mode_dev
     pool_rows = owners * per_batch + ranking
     source_rows = jnp.take(pool_rows, pair_src, axis=0)
@@ -98,19 +109,232 @@
     return (solution, forcing - coupled)
 
 
+def split3(x):
+    hi = x.astype(jnp.bfloat16)
+    rest = x - hi.astype(jnp.float32)
+    mid = rest.astype(jnp.bfloat16)
+    low = (rest - mid.astype(jnp.float32)).astype(jnp.bfloat16)
+    return hi, mid, low
+
+
+def sweep_kernel(
+    dims, f_ref, a_ref, inv_ref, w_ref, sol_ref, r_ref, ax, ay, ex, ey, dvx, dvy, w6, a6x, a6y
+):
+    batches, sources, modes, width, steps, cells, rows = dims
+    blocks = modes // 8
+    a = a_ref[...]
+    for a6, shift in ((a6x, width), (a6y, 1)):
+        hi, mid, low = split3(a + pltpu.roll(a, cells - shift, 1))
+        a6[...] = jnp.concatenate([hi, mid, low, hi, mid, hi], axis=0)
+    chunk = 2 * LANES
+    for c in range(batches):
+        hi, mid, low = split3(0.5 * w_ref[c])
+        w6[...] = jnp.concatenate([hi, hi, hi, mid, mid, low], axis=1)
+
+        @pl.loop(0, cells // chunk)
+        def _(n):
+            at = pl.ds(pl.multiple_of(n * chunk, chunk), chunk)
+            ax[c, :, at] = jnp.dot(w6[...], a6x[:, at], preferred_element_type=jnp.float32)
+            ay[c, :, at] = jnp.dot(w6[...], a6y[:, at], preferred_element_type=jnp.float32)
+
+    r_ref[...] = f_ref[...]
+    sol_ref[...] = jnp.zeros_like(sol_ref)
+    ex[...] = jnp.zeros_like(ex)
+    ey[...] = jnp.zeros_like(ey)
+    for k in range(steps):
+        c = k % batches
+        mine = pl.ds(c * sources, sources)
+        u = r_ref[mine, :] * inv_ref[...]
+        sol_ref[mine, :] = sol_ref[mine, :] + u
+        dvx[...] = u - pltpu.roll(u, cells - width, 1)
+        dvy[...] = u - pltpu.roll(u, cells - 1, 1)
+        first = (width * k) // LANES
+        last = -(-(width * (rows - 1 - k)) // LANES)
+
+        @pl.loop(first, last)
+        def _(g):
+            at = pl.ds(pl.multiple_of(g * LANES, LANES), LANES)
+            for table, diff, out in ((ax, dvx, ex), (ay, dvy, ey)):
+                sums = [None] * blocks
+                for s in range(sources):
+                    d = jnp.broadcast_to(diff[pl.ds(s, 1), at], (8, LANES))
+                    for b in range(blocks):
+                        term = table[c, pl.ds(s * modes + b * 8, 8), at] * d
+                        sums[b] = term if s == 0 else sums[b] + term
+                for b in range(blocks):
+                    out[pl.ds(b * 8, 8), at] = sums[b]
+
+        for b in range(blocks):
+            some = pl.ds(b * 8, 8)
+            x = ex[some, :]
+            y = ey[some, :]
+            div = (x - pltpu.roll(x, width, 1)) + (y - pltpu.roll(y, 1, 1))
+            r_ref[some, :] = r_ref[some, :] - div
+
+
+def patch_sizes(mesh, forcing, pair_src, coef_fields):
+    owners = mesh.shape["mode"]
+    modes, nx, ny = forcing.shape
+    batches = pair_src.shape[0]
+    depth = SWEEPS * batches
+    slab = nx // mesh.shape["space"]
+    cols = ny // owners
+    width = cols + 2 * depth
+    rows = slab + 2 * depth
+    cells = -(-(rows * width) // (2 * LANES)) * 2 * LANES
+    sources = modes // batches
+    table = 2 * batches * sources * modes * cells * 4
+    fits = (
+        table + 12_000_000 < VMEM_BYTES
+        and slab > depth
+        and modes % 8 == 0
+        and sources % 8 == 0
+        and ny % owners == 0
+        and coef_fields.shape[0] <= 40
+    )
+    return fits, (batches, sources, modes, width, depth, cells, rows)
+
+
+def halo_rows(block, width):
+    return with_halo(block, (("space", block.ndim - 2),), width)
+
+
+def by_patch(dims, forcing, mean_field, coef_fields, color, pair_src, pair_field, pair_value):
+    batches, sources, modes, width, depth, cells, rows = dims
+    mode_dev, slab, ny = forcing.shape
+    owners = modes // mode_dev
+    per_batch = mode_dev // batches
+    cols = ny // owners
+    fields = coef_fields.shape[0]
+    kpad = -(-fields // 8) * 8
+    nz = pair_src.shape[2]
+    me = lax.axis_index("mode")
+    ranking = ranks(color, mode_dev, batches)
+    mode_ids = jnp.arange(modes, dtype=jnp.int32)
+    pool_rows = (mode_ids // mode_dev) * per_batch + ranking
+    source_rows = jnp.sum(
+        jnp.where(pair_src[..., None] == mode_ids, pool_rows, 0), axis=-1, dtype=jnp.int32
+    )
+    slot = color * per_batch + ranking
+    local_slot = lax.dynamic_slice_in_dim(slot, me * mode_dev, mode_dev)
+    slots = jnp.arange(mode_dev, dtype=jnp.int32)
+    pick = slots[:, None] == local_slot[None, :]
+
+    def reorder(x, table):
+        return sum(
+            jnp.where(
+                table[:, j].reshape((-1,) + (1,) * (x.ndim - 1)), x[j][None], jnp.float32(0)
+            )
+            for j in range(mode_dev)
+        )
+
+    def windows(x):
+        padded = jnp.pad(x, ((0, 0), (0, 0), (depth, depth)))
+        return jnp.stack(
+            [padded[:, :, m * cols : m * cols + width] for m in range(owners)], axis=0
+        )
+
+    ordered = reorder(forcing, pick)
+    out = windows(halo_rows(ordered, depth)).reshape(owners, mode_dev, rows * width)
+    out = jnp.pad(out, ((0, 0), (0, 0), (0, cells - rows * width)))
+    key = (source_rows * kpad + pair_field).astype(jnp.float32)
+    both = jnp.stack([key, pair_value], axis=0)
+    both = reorder(both.transpose(2, 0, 1, 3), pick).reshape(-1)
+    extra = -(-both.shape[0] // cells)
+    both = jnp.pad(both, (0, extra * cells - both.shape[0])).reshape(1, extra, cells)
+    out = jnp.concatenate([out, jnp.broadcast_to(both, (owners, extra, cells))], axis=1)
+    got = lax.all_to_all(out, "mode", 0, 0, tiled=True)
+    values = got[:, :mode_dev].reshape(owners, batches, per_batch, cells)
+    values = values.transpose(1, 0, 2, 3).reshape(modes, cells)
+    entries = got[:, mode_dev:].reshape(owners, extra * cells)
+    entries = entries[:, : mode_dev * 2 * batches * nz].reshape(
+        owners, batches, per_batch, 2, batches, nz
+    )
+    entries = entries.transpose(3, 4, 1, 0, 2, 5).reshape(2, batches, modes, nz)
+    keys = entries[0].astype(jnp.int32)
+    places = jnp.arange(sources * kpad, dtype=jnp.int32)
+    dense = jnp.zeros((batches, modes, sources * kpad), jnp.float32)
+    for z in range(nz):
+        dense = dense + jnp.where(keys[:, :, z, None] == places, entries[1][:, :, z, None], 0.0)
+    dense = dense.reshape(batches, modes, sources, kpad).transpose(0, 2, 1, 3)
+    dense = dense.reshape(batches, sources * modes, kpad)
+
+    def window(x, margin):
+        padded = jnp.pad(x, ((0, 0), (0, 0), (margin, margin)))
+        return lax.dynamic_slice_in_dim(padded, me * cols, cols + 2 * margin, axis=2)
+
+    coef = halo_rows(window(coef_fields, depth), depth).reshape(fields, rows * width)
+    coef = jnp.pad(coef, ((0, kpad - fields), (0, cells - rows * width)))
+    mean = halo_rows(window(mean_field[None], depth + 1), depth + 1)[0]
+    mid = mean[1:-1, 1:-1]
+    diag = 0.5 * (
+        4.0 * mid + mean[2:, 1:-1] + mean[:-2, 1:-1] + mean[1:-1, 2:] + mean[1:-1, :-2]
+    )
+    row_ids = lax.axis_index("space") * slab - depth + jnp.arange(rows)
+    col_ids = me * cols - depth + jnp.arange(width)
+    total_rows = slab * lax.axis_size("space")
+    inside = ((row_ids >= 0) & (row_ids < total_rows))[:, None] & (
+        (col_ids >= 0) & (col_ids < ny)
+    )[None, :]
+    inv = jnp.where(inside, 1.0 / jnp.where(inside, diag, 1.0), 0.0).reshape(1, rows * width)
+    inv = jnp.pad(inv, ((0, 0), (0, cells - rows * width)))
+
+    patch = jax.ShapeDtypeStruct((modes, cells), jnp.float32)
+    vmem = pl.BlockSpec(memory_space=pltpu.VMEM)
+    table = pltpu.VMEM((batches, sources * modes, cells), jnp.float32)
+    state = pltpu.VMEM((modes, cells), jnp.float32)
+    diff = pltpu.VMEM((sources, cells), jnp.float32)
+    coef6 = pltpu.VMEM((6 * kpad, cells), jnp.bfloat16)
+    sol, res = pl.pallas_call(
+        functools.partial(sweep_kernel, dims),
+        out_shape=(patch, patch),
+        in_specs=[vmem] * 4,
+        out_specs=(vmem, vmem),
+        scratch_shapes=[
+            table,
+            table,
+            state,
+            state,
+            diff,
+            diff,
+            pltpu.VMEM((sources * modes, 6 * kpad), jnp.bfloat16),
+            coef6,
+            coef6,
+        ],
+        compiler_params=pltpu.CompilerParams(vmem_limit_bytes=VMEM_BYTES),
+        name="sweeps",
+    )(values, coef, inv, dense)
+
+    done = jnp.stack([sol, res], axis=0)[:, :, : rows * width]
+    done = done.reshape(2, batches, owners, per_batch, rows, width)
+    done = done[..., depth : depth + slab, depth : depth + cols]
+    done = done.transpose(2, 0, 1, 3, 4, 5).reshape(owners, 2 * mode_dev * slab * cols)
+    back = lax.all_to_all(done, "mode", 0, 0, tiled=True)
+    back = back.reshape(owners, 2, mode_dev, slab, cols).transpose(2, 1, 3, 0, 4)
+    back = reorder(back.reshape(mode_dev, 2, slab, ny), pick.T)
+    return back[:, 0], back[:, 1]
+
+
 def solution(mesh):
-    return jax.shard_map(
-        on_device,
-        mesh=mesh,
-        in_specs=(
-            P("mode", "space", None),
-            P("space", None),
-            P(None, "space", None),
-            P(),
-            P(None, "mode", None),
-            P(None, "mode", None),
-            P(None, "mode", None),
-        ),
-        out_specs=(P("mode", "space", None), P("mode", "space", None)),
-        check_vma=False,
-    )
+    specs = (
+        P("mode", "space", None),
+        P("space", None),
+        P(None, "space", None),
+        P(),
+        P(None, "mode", None),
+        P(None, "mode", None),
+        P(None, "mode", None),
+    )
+
+    def whole(*args):
+        fits, dims = patch_sizes(mesh, args[0], args[4], args[2])
+        body = functools.partial(by_patch, dims) if fits else by_batch
+        return jax.shard_map(
+            body,
+            mesh=mesh,
+            in_specs=specs,
+            out_specs=(P("mode", "space", None), P("mode", "space", None)),
+            check_vma=False,
+        )(*args)
+
+    return whole

time: 518 us -> 144 us (0.28)
  blocking collectives: 248 us -> 13.5 us
  local copies, waits for them, and re-layouts: 134 us -> 24.9 us
  other arithmetic: 65.5 us -> 34.3 us
  Pallas kernels: 0 us -> 29.1 us
  waiting for transfers between devices: 34.5 us -> 18.6 us
  loops' own time: 5.91 us -> 0 us
    all_gather x8 -> x0, blocking collectives: 248 us -> none  [on_device(): inner = lax.all_gather(own_update, 'mode', axis=0, tiled=True)]
    gather x138 -> x0, local copies, waits for them, and re-layouts: 84.4 us -> none  [the longest x64 37.6 us: reader(): values = jnp.take(gathered, source_rows, axis=0)]
    reduce_sum x66 -> x2, other arithmetic: 38.8 us -> 1.48 us  [the longest x1 1.47 us: by_patch(): jnp.sum(jnp.where(pair_src[..., None] == mode_ids, pool_rows, 0), axis=-1...]
    ppermute x9 -> x3, waiting for transfers between devices: 34.4 us -> 0.01 us  [with_halo(): lax.ppermute(lax.slice_in_dim(block, 0, width, axis=dim), axis, backward)]
    pallas_call x0 -> x1, Pallas kernels: none -> 29.1 us  [by_patch(): pl.pallas_call(functools.partial(sweep_kernel, dims), out_shape=(patch, p...]
    mul x64 -> x0, local copies, waits for them, and re-layouts: 27.8 us -> none  [reader(): return jnp.sum(weight_rows[:, None, None] * fluxes, axis=0)]
    add x3 -> x5, other arithmetic: 1.89 us -> 28.5 us  [the longest x1 27.4 us: by_patch(): dense + jnp.where(keys[:, :, z, None] == places, entries[1][:, :, z, None...]
    select_n x149 -> x1, other arithmetic: 19.5 us -> 0.09 us  [by_patch(): jnp.where(inside, 1.0 / jnp.where(inside, diag, 1.0), 0.0)]
  transfers between devices with their start and end apart: 18 -> 7, of which waited for: 8 -> 1; matrix products, arithmetic and copies ran while one was open for 2% -> 9% of each run, Pallas kernels for 0% -> 0%
where the time goes in v1:
time: 144 us; the launch traced here: 143 us
  other arithmetic  34.3 us (24%)
  Pallas kernels  29.1 us (20%)
  local copies, waits for them, and re-layouts  24.9 us (17%)
  starting transfers between devices  21.4 us (15%)
  waiting for transfers between devices  18.6 us (13%)
  blocking collectives  13.5 us (9%)
    pallas_call x1, Pallas kernels, by_patch(): pl.pallas_call(functools.partial(sweep_kernel, dims), out_shape=(patch, p...  29.1 us
    add x1, other arithmetic, by_patch(): dense + jnp.where(keys[:, :, z, None] == places, entries[1][:, :, z, None...  27.4 us
    all_to_all x1, waiting for transfers between devices, by_patch(): got = lax.all_to_all(out, 'mode', 0, 0, tiled=True)  18.5 us
    all_to_all x1, blocking collectives, by_patch(): back = lax.all_to_all(done, 'mode', 0, 0, tiled=True)  13.5 us
    ppermute x3, starting transfers between devices, with_halo(): lax.ppermute(lax.slice_in_dim(block, block.shape[dim] - width, None, axis...  11.8 us
    all_to_all x1, starting transfers between devices, by_patch(): got = lax.all_to_all(out, 'mode', 0, 0, tiled=True)  5.67 us
    ppermute x3, starting transfers between devices, with_halo(): lax.ppermute(lax.slice_in_dim(block, 0, width, axis=dim), axis, backward)  3.88 us
    another operation x2, local copies, waits for them, and re-layouts, by_patch(): done = jnp.stack([sol, res], axis=0)[:, :, :rows * width]  2.89 us
  transfers between devices with their start and end apart: 7, of which 1 were waited for; matrix products, arithmetic and copies ran while one was open for 9% of the time, Pallas kernels for 0%

profile of v1, /device:TPU:0, one launch (start us, length us, event | category | flops | bytes accessed | tf_op | source)
XLA Modules:
  0.0 143.0 jit_solution(10348125759158573218)
XLA Ops:
  0.6 0.9 pad_dynamic-slice_fusion.4
  1.5 2.4 %collective-permute-start.4 = (f32[1,9,50]{2,1,0:T(8,128)S(1)}, f32[1,9,50]{2,1,0:T(8,128)S(1)}, u32[]{:S(2)}, u32[]{:S(2)}) collective-permute-start(f32[1,9,50]{2,1,0:T(8,128)S(1)} %get-tuple-element.94), channel_id=1, source_target_pairs={{0,1},{1,2},{2,3},{4,5},{5,6},{6,7},{8,9},{9,10},{10,11},{12,13},{... | collective-permute-start | bytes 5408 | tf_op jit(solution)/shard_map/ppermute | solution.py:21
  3.9 1.3 collective-permute-start.5
  5.2 0.7 eq.771
  6.0 0.7 reduce_window_sum.11
  6.7 0.7 multiply_add_fusion.1
  7.5 0.8 slice_bitcast_fusion.9
  8.4 0.1 select_add_fusion.2
  8.6 5.2 %collective-permute-start = (f32[8,8,256]{2,1,0:T(8,128)S(1)}, f32[8,8,256]{2,1,0:T(8,128)S(1)}, u32[]{:S(2)}, u32[]{:S(2)}) collective-permute-start(f32[8,8,256]{2,1,0:T(8,128)S(1)} %get-tuple-element.76), channel_id=1, source_target_pairs={{0,1},{1,2},{2,3},{4,5},{5,6},{6,7},{8,9},{9,10},{10,11},{12,13},{... | collective-permute-start | bytes 196616 | tf_op jit(solution)/shard_map/ppermute | solution.py:21
  13.7 1.3 collective-permute-start.1
  15.0 1.2 pad_dynamic-slice_fusion.1
  16.2 4.3 %collective-permute-start.2 = (f32[28,8,48]{2,1,0:T(8,128)S(1)}, f32[28,8,48]{2,1,0:T(8,128)S(1)}, u32[]{:S(2)}, u32[]{:S(2)}) collective-permute-start(f32[28,8,48]{2,1,0:T(8,128)S(1)} %get-tuple-element.62), channel_id=1, source_target_pairs={{0,1},{1,2},{2,3},{4,5},{5,6},{6,7},{8,9},{9,10},{10,11},{12,13},{... | collective-permute-start | bytes 129032 | tf_op jit(solution)/shard_map/ppermute | solution.py:21
  20.5 0.8 pad_dynamic-slice_fusion.5
  21.3 1.5 %select_reduce_fusion = s32[4,8,24]{2,1,0:T(8,128)S(1)} fusion(s32[64]{0:T(128)S(1)} %get-tuple-element.115, s32[4,8,24]{2,1,0:T(8,128)} %param.11), kind=kLoop, calls=%fused_computation.10 | loop fusion | flops 146688 | bytes 6400 | tf_op jit(solution)/shard_map/reduce_sum | solution.py:215
  22.8 0.7 convert_bitcast_fusion
  23.5 0.7 maximum_bitcast_fusion
  24.3 0.1 add_add_fusion
  24.5 1.3 collective-permute-start.3
  25.9 0.3 pad_slice_fusion
  27.3 1.0 pad_maximum_fusion.1
  28.2 5.7 %all-to-all-start = ((f32[8,9,1536]{2,1,0:T(8,128)}), f32[8,9,1536]{2,1,0:T(8,128)S(1)}, u32[]{:S(2)}, u32[]{:S(2)}) async-start(f32[8,9,1536]{2,1,0:T(8,128)} %pad_maximum_fusion.1), calls=%async_computation | async-start | bytes 1572864 | tf_op jit(solution)/shard_map/all_to_all | solution.py:246
  33.9 0.1 pad_dynamic-slice_fusion.2
  34.2 0.7 reshape.350.inv_ref
  35.0 0.2 reshape.349
  35.2 0.7 pad.18.a_ref
  35.9 18.5 %all-to-all-done = f32[8,9,1536]{2,1,0:T(8,128)S(1)} async-done(((f32[8,9,1536]{2,1,0:T(8,128)}), f32[8,9,1536]{2,1,0:T(8,128)S(1)}, u32[]{:S(2)}, u32[]{:S(2)}) %all-to-all-start) | async-done | bytes 442400 | tf_op jit(solution)/shard_map/all_to_all | solution.py:246
  54.4 0.1 slice_reduce_fusion.48
  54.5 0.4 reshape_reshape.3
  54.9 0.2 copy.78
  55.2 0.6 slice_reduce_fusion.45
  55.8 2.0 %slice_reduce_fusion.47 = (s32[4,64]{1,0:T(4,128)S(1)}, s32[4,64]{1,0:T(4,128)S(1)}, s32[4,64]{1,0:T(4,128)S(1)}, s32[4,64]{1,0:T(4,128)S(1)}, s32[4,64]{1,0:T(4...) fusion(s32[4,64,24]{2,1,0:T(8,128)S(1)} %bitcast.99), kind=kLoop, calls=%fused_computation.64 | loop fusion | bytes 38912 | tf_op jit(solution)/shard_map/slice | solution.py:258
  57.9 0.5 slice_reduce_fusion.44
  58.4 1.4 slice_reduce_fusion.46
  59.8 0.2 copy.74
  60.0 0.3 copy.58
  60.3 1.0 reshape.348.f_ref
  65.7 27.4 %select_add_fusion.w_ref = f32[4,1024,32]{2,1,0:T(8,128)} fusion(f32[4,1024]{1,0:T(4,128)S(1)} %broadcast_in_dim.877, s32[4,1024]{1,0:T(4,128)S(1)} %eq.906, f32[4,1024]{1,0:T(4,128)S(1)} %broadcast_in_dim.873, s32[4,1024]{1,0:T(4,128)S(1)} %eq.901, f32[4,1024]{1,0:T(4,128)S(1)} %broadcast_in_dim.869, s32[4,1024]{1,0:T(4,128)S(1)} %eq.896, ...), kind=kLoop, calls=%fused_computation | loop fusion | flops 9306112 | bytes 1441792 | tf_op jit(solution)/shard_map/add | solution.py:258
  93.1 29.1 %sweeps.1 = (f32[64,1536]{1,0:T(8,128)}, f32[64,1536]{1,0:T(8,128)}) custom-call(f32[64,1536]{1,0:T(8,128)} %reshape.348.f_ref, f32[32,1536]{1,0:T(8,128)} %pad.18.a_ref, f32[1,1536]{1,0:T(1,128)} %reshape.350.inv_ref, f32[4,1024,32]{2,1,0:T(8,128)} %select_add_fusion.w_ref), custom_call_target="tpu_custom_call" | custom-call | tf_op jit(solution)/shard_map/sweeps/pallas_call | solution.py:288
  122.2 1.4 %stack.57 = f32[1,4,8,2,32,48]{5,4,3,2,1,0:T(8,128)S(1)} reshape(f32[64,1536]{1,0:T(8,128)} %get-tuple-element.4) | data formatting | bytes 786432 | tf_op jit(solution)/shard_map/stack | solution.py:308
  123.7 1.4 %stack.58 = f32[1,4,8,2,32,48]{5,4,3,2,1,0:T(8,128)S(1)} reshape(f32[64,1536]{1,0:T(8,128)} %get-tuple-element.5) | data formatting | bytes 786432 | tf_op jit(solution)/shard_map/stack | solution.py:308
  125.1 0.3 copy_bitcast_fusion
  125.5 0.5 all_to_all.12
  125.9 13.5 %all_to_all.15 = f32[8,1,8192]{2,1,0:T(1,128)S(1)} all-to-all(f32[8,1,8192]{2,1,0:T(1,128)S(1)} %all_to_all.12), channel_id=1, replica_groups=mesh['mode'=8,'space'=4] {'mode'}, dimensions={0} | all-to-all | bytes 524288 | tf_op jit(solution)/shard_map/all_to_all | solution.py:312
  139.5 0.6 reduce.49
  140.1 0.3 reshape.351
  140.4 0.1 fusion.5
  142.0 0.2 select_add_fusion.1
  142.3 0.7 slice_bitcast_fusion
  (158 shorter events, 7.5 us)
Async XLA Ops:
  1.5 32.6 %collective-permute-start.4 = (f32[1,9,50]{2,1,0:T(8,128)S(1)}, f32[1,9,50]{2,1,0:T(8,128)S(1)}, u32[]{:S(2)}, u32[]{:S(2)}) collective-permute-start(f32[1,9,50]{2,1,0:T(8,128)S(1)} %get-tuple-element.94), channel_id=1, source_target_pairs={{0,1},{1,2},{2,3},{4,5},{5,6},{6,7},{8,9},{9,10},{10,11},{12,13},{... | collective-permute-start | bytes 5408 | tf_op jit(solution)/shard_map/ppermute | solution.py:21
  3.9 30.2 %collective-permute-start.5 = (f32[1,9,50]{2,1,0:T(8,128)S(1)}, f32[1,9,50]{2,1,0:T(8,128)S(1)}, u32[]{:S(2)}, u32[]{:S(2)}) collective-permute-start(f32[1,9,50]{2,1,0:T(8,128)S(1)} %get-tuple-element.95), channel_id=1, source_target_pairs={{1,0},{2,1},{3,2},{5,4},{6,5},{7,6},{9,8},{10,9},{11,10},{13,12},{... | collective-permute-start | bytes 5408 | tf_op jit(solution)/shard_map/ppermute | solution.py:24
  8.6 16.0 %collective-permute-start = (f32[8,8,256]{2,1,0:T(8,128)S(1)}, f32[8,8,256]{2,1,0:T(8,128)S(1)}, u32[]{:S(2)}, u32[]{:S(2)}) collective-permute-start(f32[8,8,256]{2,1,0:T(8,128)S(1)} %get-tuple-element.76), channel_id=1, source_target_pairs={{0,1},{1,2},{2,3},{4,5},{5,6},{6,7},{8,9},{9,10},{10,11},{12,13},{... | collective-permute-start | bytes 196616 | tf_op jit(solution)/shard_map/ppermute | solution.py:21
  13.7 12.1 %collective-permute-start.1 = (f32[8,8,256]{2,1,0:T(8,128)S(1)}, f32[8,8,256]{2,1,0:T(8,128)S(1)}, u32[]{:S(2)}, u32[]{:S(2)}) collective-permute-start(f32[8,8,256]{2,1,0:T(8,128)S(1)} %get-tuple-element.77), channel_id=1, source_target_pairs={{1,0},{2,1},{3,2},{5,4},{6,5},{7,6},{9,8},{10,9},{11,10},{13,12},{... | collective-permute-start | bytes 196616 | tf_op jit(solution)/shard_map/ppermute | solution.py:24
  16.2 18.7 %collective-permute-start.2 = (f32[28,8,48]{2,1,0:T(8,128)S(1)}, f32[28,8,48]{2,1,0:T(8,128)S(1)}, u32[]{:S(2)}, u32[]{:S(2)}) collective-permute-start(f32[28,8,48]{2,1,0:T(8,128)S(1)} %get-tuple-element.62), channel_id=1, source_target_pairs={{0,1},{1,2},{2,3},{4,5},{5,6},{6,7},{8,9},{9,10},{10,11},{12,13},{... | collective-permute-start | bytes 129032 | tf_op jit(solution)/shard_map/ppermute | solution.py:21
  24.5 10.4 %collective-permute-start.3 = (f32[28,8,48]{2,1,0:T(8,128)S(1)}, f32[28,8,48]{2,1,0:T(8,128)S(1)}, u32[]{:S(2)}, u32[]{:S(2)}) collective-permute-start(f32[28,8,48]{2,1,0:T(8,128)S(1)} %get-tuple-element.63), channel_id=1, source_target_pairs={{1,0},{2,1},{3,2},{5,4},{6,5},{7,6},{9,8},{10,9},{11,10},{13,12},{... | collective-permute-start | bytes 129032 | tf_op jit(solution)/shard_map/ppermute | solution.py:24
  26.8 7.1 %copy-start = (f32[28,16,256]{2,1,0:T(8,128)S(1)}, f32[28,16,256]{2,1,0:T(8,128)}, u32[]{:S(2)}) copy-start(f32[28,16,256]{2,1,0:T(8,128)} %param.9) | copy-start | bytes 1376260
  28.2 26.2 %all-to-all-start = ((f32[8,9,1536]{2,1,0:T(8,128)}), f32[8,9,1536]{2,1,0:T(8,128)S(1)}, u32[]{:S(2)}, u32[]{:S(2)}) async-start(f32[8,9,1536]{2,1,0:T(8,128)} %pad_maximum_fusion.1), calls=%async_computation | async-start | bytes 1572864 | tf_op jit(solution)/shard_map/all_to_all | solution.py:246

commit v2 on v1

--- a/solution.py
+++ b/solution.py
@@ -110,26 +110,165 @@
 
 
 def split3(x):
-    hi = x.astype(jnp.bfloat16)
-    rest = x - hi.astype(jnp.float32)
-    mid = rest.astype(jnp.bfloat16)
-    low = (rest - mid.astype(jnp.float32)).astype(jnp.bfloat16)
-    return hi, mid, low
-
-
-def sweep_kernel(
-    dims, f_ref, a_ref, inv_ref, w_ref, sol_ref, r_ref, ax, ay, ex, ey, dvx, dvy, w6, a6x, a6y
-):
-    batches, sources, modes, width, steps, cells, rows = dims
+    hi = x.astype(jnp.bfloat16).astype(jnp.float32)
+    mid = (x - hi).astype(jnp.bfloat16).astype(jnp.float32)
+    return hi, mid, x - hi - mid
+
+
+def sweep_kernel(dims, win, pairs, cw, back, ax, ay, r, sol, ex, ey, dvx, dvy, w6, a6x, a6y,
+                 allp, cbuf, inv, dense, send, recv, hsend, hrecv, csend, crecv):
+    batches, sources, modes, width, steps, cells, rows, fields, nz, owners, slabs = dims
+    mode_dev = modes // owners
+    per_batch = mode_dev // batches
     blocks = modes // 8
-    a = a_ref[...]
+    edge = width * steps
+    core_cells = cells - 2 * edge
+    me = lax.axis_index("mode")
+    slab = lax.axis_index("space")
+    low, mid_at, high = pl.ds(0, edge), pl.ds(edge, core_cells), pl.ds(cells - edge, edge)
+
+    def owner_rows(o):
+        return pl.ds(pl.multiple_of(o * mode_dev, mode_dev), mode_dev)
+
+    def remote(src, dst, ssem, rsem, **where):
+        return pltpu.make_async_remote_copy(
+            src_ref=src, dst_ref=dst, send_sem=ssem, recv_sem=rsem, device_id=where,
+            device_id_type=pl.DeviceIdType.MESH,
+        )
+
+    has_low, has_high = slab > 0, slab < slabs - 1
+    barrier = pltpu.get_barrier_semaphore()
+    for d in range(1, owners):
+        pl.semaphore_signal(
+            barrier, inc=1, device_id={"mode": lax.rem(me + d, owners)},
+            device_id_type=pl.DeviceIdType.MESH,
+        )
+    for there, at in ((has_low, slab - 1), (has_high, slab + 1)):
+
+        @pl.when(there)
+        def _():
+            pl.semaphore_signal(
+                barrier, inc=1, device_id={"space": at}, device_id_type=pl.DeviceIdType.MESH
+            )
+
+    beside = has_low.astype(jnp.int32) + has_high.astype(jnp.int32)
+    pl.semaphore_wait(barrier, owners - 1 + beside)
+
+    def peer(d):
+        return lax.rem(me + d, owners)
+
+    def origin(d):
+        return lax.rem(me + owners - d, owners)
+
+    def pair_copy(d, o):
+        return remote(pairs, allp.at[owner_rows(o)], send.at[0, d], recv.at[0, d], mode=peer(d))
+
+    def value_copy(d, o):
+        return remote(
+            win.at[peer(d)], r.at[owner_rows(o), mid_at], send.at[1, d], recv.at[1, d],
+            mode=peer(d),
+        )
+
+    def up_copy(d, o):
+        return remote(
+            r.at[owner_rows(o), pl.ds(core_cells, edge)], r.at[owner_rows(o), low],
+            hsend.at[0, d], hrecv.at[0, d], space=slab + 1,
+        )
+
+    def down_copy(d, o):
+        return remote(
+            r.at[owner_rows(o), pl.ds(edge, edge)], r.at[owner_rows(o), high],
+            hsend.at[1, d], hrecv.at[1, d], space=slab - 1,
+        )
+
+    def coef_up():
+        return remote(
+            cw.at[:, pl.ds(core_cells - edge, edge)], cbuf.at[:, low], csend.at[0], crecv.at[0],
+            space=slab + 1,
+        )
+
+    def coef_down():
+        return remote(
+            cw.at[:, pl.ds(0, edge)], cbuf.at[:, high], csend.at[1], crecv.at[1], space=slab - 1
+        )
+
+    for d in range(1, owners):
+        pair_copy(d, me).start()
+    pl.when(has_high)(lambda: coef_up().start())
+    pl.when(has_low)(lambda: coef_down().start())
+    for d in range(1, owners):
+        value_copy(d, me).start()
+
+    allp[owner_rows(me), :] = pairs[...]
+    r[owner_rows(me), mid_at] = win[me]
+    cbuf[:, mid_at] = cw[...]
+    for there, at in ((has_low, low), (has_high, high)):
+
+        @pl.when(jnp.logical_not(there))
+        def _():
+            r[:, at] = jnp.zeros((modes, edge), jnp.float32)
+            cbuf[:, at] = jnp.zeros((cbuf.shape[0], edge), jnp.float32)
+
+    sol[...] = jnp.zeros_like(sol)
+    ex[...] = jnp.zeros_like(ex)
+    ey[...] = jnp.zeros_like(ey)
+
+    pl.when(has_high)(lambda: coef_up().wait_send())
+    pl.when(has_low)(lambda: coef_down().wait_send())
+    pl.when(has_low)(lambda: coef_up().wait_recv())
+    pl.when(has_high)(lambda: coef_down().wait_recv())
+    a = cbuf[...]
+    kpad = a.shape[0]
     for a6, shift in ((a6x, width), (a6y, 1)):
-        hi, mid, low = split3(a + pltpu.roll(a, cells - shift, 1))
-        a6[...] = jnp.concatenate([hi, mid, low, hi, mid, hi], axis=0)
+        parts = split3(0.5 * (a + pltpu.roll(a, cells - shift, 1)))
+        hi, mid, rest = [x.astype(jnp.bfloat16) for x in parts]
+        none = jnp.zeros_like(hi)
+        a6[...] = jnp.concatenate([hi, mid, rest, hi, mid, hi, none, none], axis=0)
+    extra = a[fields : fields + 4]
+    place = lax.broadcasted_iota(jnp.int32, (1, cells), 1)
+    centre, across = extra[1:2], extra[0:1]
+    above = jnp.where(place < width, extra[2:3], pltpu.roll(centre, width, 1))
+    below = jnp.where(
+        place >= width * (rows - 1), extra[3:4], pltpu.roll(centre, cells - width, 1)
+    )
+    inside = across > 0.0
+    diag = jnp.where(inside, 0.5 * (across + above + below), 1.0)
+    inv[...] = jnp.where(inside, 1.0 / diag, 0.0)
+
+    for d in range(1, owners):
+        pair_copy(d, me).wait_send()
+        pair_copy(d, me).wait_recv()
+
     chunk = 2 * LANES
-    for c in range(batches):
-        hi, mid, low = split3(0.5 * w_ref[c])
-        w6[...] = jnp.concatenate([hi, hi, hi, mid, mid, low], axis=1)
+    per_group = LANES // kpad
+    lane = lax.broadcasted_iota(jnp.int32, (8, LANES), 1)
+    lane_f = lane.astype(jnp.float32)
+    value_lane = allp.shape[1] // 2
+
+    def build(c):
+        @pl.loop(0, blocks)
+        def _(b):
+            own = allp[pl.ds(pl.multiple_of(b * 8, 8), 8), :]
+            sums = [jnp.zeros((8, LANES), jnp.float32)] * (sources // per_group)
+            for z in range(nz):
+                e = c * nz + z
+                key = jnp.broadcast_to(own[:, e : e + 1], (8, LANES))
+                val = jnp.broadcast_to(own[:, value_lane + e : value_lane + e + 1], (8, LANES))
+                for g in range(sources // per_group):
+                    sums[g] = sums[g] + jnp.where(key == lane_f + float(g * LANES), val, 0.0)
+            for g in range(sources // per_group):
+                for j in range(per_group):
+                    one = jnp.where((lane >= j * kpad) & (lane < (j + 1) * kpad), sums[g], 0.0)
+                    one = one + pltpu.roll(one, kpad, 1)
+                    one = one + pltpu.roll(one, 2 * kpad, 1)
+                    hi, mid, rest = split3(one)
+                    first = jnp.where(lane < 3 * kpad, hi, mid)
+                    second = jnp.where(lane < kpad, mid, jnp.where(lane < 2 * kpad, rest, 0.0))
+                    at = pl.ds(pl.multiple_of((g * per_group + j) * modes + b * 8, 8), 8)
+                    dense[at, pl.ds(0, LANES)] = first
+                    dense[at, pl.ds(LANES, LANES)] = second
+
+        w6[...] = dense[...].astype(jnp.bfloat16)
 
         @pl.loop(0, cells // chunk)
         def _(n):
@@ -137,17 +276,41 @@
             ax[c, :, at] = jnp.dot(w6[...], a6x[:, at], preferred_element_type=jnp.float32)
             ay[c, :, at] = jnp.dot(w6[...], a6y[:, at], preferred_element_type=jnp.float32)
 
-    r_ref[...] = f_ref[...]
-    sol_ref[...] = jnp.zeros_like(sol_ref)
-    ex[...] = jnp.zeros_like(ex)
-    ey[...] = jnp.zeros_like(ey)
+    build(0)
+    for d in range(owners):
+        if d:
+            value_copy(d, me).wait_send()
+            value_copy(d, me).wait_recv()
+        pl.when(has_high)(lambda: up_copy(d, origin(d)).start())
+        pl.when(has_low)(lambda: down_copy(d, origin(d)).start())
+    for c in range(1, batches):
+        build(c)
+    for d in range(owners):
+        pl.when(has_high)(lambda: up_copy(d, origin(d)).wait_send())
+        pl.when(has_low)(lambda: down_copy(d, origin(d)).wait_send())
+        pl.when(has_low)(lambda: up_copy(d, origin(d)).wait_recv())
+        pl.when(has_high)(lambda: down_copy(d, origin(d)).wait_recv())
+
+    def out_copy(which, src, d):
+        return remote(
+            src.at[owner_rows(peer(d)), mid_at], back.at[which, me], send.at[2 + which, d],
+            recv.at[2 + which, d], mode=peer(d),
+        )
+
     for k in range(steps):
         c = k % batches
-        mine = pl.ds(c * sources, sources)
-        u = r_ref[mine, :] * inv_ref[...]
-        sol_ref[mine, :] = sol_ref[mine, :] + u
+        pieces = []
+        for o in range(owners):
+            mine = pl.ds(o * mode_dev + c * per_batch, per_batch)
+            u = r[mine, :] * inv[...]
+            sol[mine, :] = sol[mine, :] + u
+            pieces.append(u)
+        u = jnp.concatenate(pieces, axis=0)
         dvx[...] = u - pltpu.roll(u, cells - width, 1)
         dvy[...] = u - pltpu.roll(u, cells - 1, 1)
+        if k == steps - 1:
+            for d in range(1, owners):
+                out_copy(0, sol, d).start()
         first = (width * k) // LANES
         last = -(-(width * (rows - 1 - k)) // LANES)
 
@@ -157,9 +320,9 @@
             for table, diff, out in ((ax, dvx, ex), (ay, dvy, ey)):
                 sums = [None] * blocks
                 for s in range(sources):
-                    d = jnp.broadcast_to(diff[pl.ds(s, 1), at], (8, LANES))
+                    dv = jnp.broadcast_to(diff[pl.ds(s, 1), at], (8, LANES))
                     for b in range(blocks):
-                        term = table[c, pl.ds(s * modes + b * 8, 8), at] * d
+                        term = table[c, pl.ds(s * modes + b * 8, 8), at] * dv
                         sums[b] = term if s == 0 else sums[b] + term
                 for b in range(blocks):
                     out[pl.ds(b * 8, 8), at] = sums[b]
@@ -169,45 +332,54 @@
             x = ex[some, :]
             y = ey[some, :]
             div = (x - pltpu.roll(x, width, 1)) + (y - pltpu.roll(y, 1, 1))
-            r_ref[some, :] = r_ref[some, :] - div
+            r[some, :] = r[some, :] - div
+
+    for d in range(1, owners):
+        out_copy(1, r, d).start()
+    for which, src in ((0, sol), (1, r)):
+        back[which, me] = src[owner_rows(me), mid_at]
+    for which, src in ((0, sol), (1, r)):
+        for d in range(1, owners):
+            out_copy(which, src, d).wait_send()
+            out_copy(which, src, d).wait_recv()
 
 
 def patch_sizes(mesh, forcing, pair_src, coef_fields):
     owners = mesh.shape["mode"]
+    slabs = mesh.shape["space"]
     modes, nx, ny = forcing.shape
     batches = pair_src.shape[0]
+    nz = pair_src.shape[2]
+    fields = coef_fields.shape[0]
     depth = SWEEPS * batches
-    slab = nx // mesh.shape["space"]
+    slab = nx // slabs
     cols = ny // owners
     width = cols + 2 * depth
     rows = slab + 2 * depth
-    cells = -(-(rows * width) // (2 * LANES)) * 2 * LANES
+    cells = rows * width
     sources = modes // batches
     table = 2 * batches * sources * modes * cells * 4
     fits = (
         table + 12_000_000 < VMEM_BYTES
         and slab > depth
-        and modes % 8 == 0
+        and cells % (2 * LANES) == 0
+        and (width * depth) % LANES == 0
+        and modes == 8 * owners
         and sources % 8 == 0
         and ny % owners == 0
-        and coef_fields.shape[0] <= 40
+        and 24 < fields + 4 <= LANES // 4
+        and batches * nz <= LANES
     )
-    return fits, (batches, sources, modes, width, depth, cells, rows)
-
-
-def halo_rows(block, width):
-    return with_halo(block, (("space", block.ndim - 2),), width)
+    return fits, (batches, sources, modes, width, depth, cells, rows, fields, nz, owners, slabs)
 
 
 def by_patch(dims, forcing, mean_field, coef_fields, color, pair_src, pair_field, pair_value):
-    batches, sources, modes, width, depth, cells, rows = dims
+    batches, sources, modes, width, depth, cells, rows, fields, nz, owners, slabs = dims
     mode_dev, slab, ny = forcing.shape
-    owners = modes // mode_dev
     per_batch = mode_dev // batches
     cols = ny // owners
-    fields = coef_fields.shape[0]
-    kpad = -(-fields // 8) * 8
-    nz = pair_src.shape[2]
+    kpad = LANES // 4
+    core_cells = slab * width
     me = lax.axis_index("mode")
     ranking = ranks(color, mode_dev, batches)
     mode_ids = jnp.arange(modes, dtype=jnp.int32)
@@ -228,90 +400,66 @@
             for j in range(mode_dev)
         )
 
-    def windows(x):
-        padded = jnp.pad(x, ((0, 0), (0, 0), (depth, depth)))
-        return jnp.stack(
-            [padded[:, :, m * cols : m * cols + width] for m in range(owners)], axis=0
-        )
-
-    ordered = reorder(forcing, pick)
-    out = windows(halo_rows(ordered, depth)).reshape(owners, mode_dev, rows * width)
-    out = jnp.pad(out, ((0, 0), (0, 0), (0, cells - rows * width)))
+    padded = jnp.pad(reorder(forcing, pick), ((0, 0), (0, 0), (depth, depth)))
+    win = jnp.stack([padded[:, :, m * cols : m * cols + width] for m in range(owners)], axis=0)
+    win = win.reshape(owners, mode_dev, core_cells)
     key = (source_rows * kpad + pair_field).astype(jnp.float32)
-    both = jnp.stack([key, pair_value], axis=0)
-    both = reorder(both.transpose(2, 0, 1, 3), pick).reshape(-1)
-    extra = -(-both.shape[0] // cells)
-    both = jnp.pad(both, (0, extra * cells - both.shape[0])).reshape(1, extra, cells)
-    out = jnp.concatenate([out, jnp.broadcast_to(both, (owners, extra, cells))], axis=1)
-    got = lax.all_to_all(out, "mode", 0, 0, tiled=True)
-    values = got[:, :mode_dev].reshape(owners, batches, per_batch, cells)
-    values = values.transpose(1, 0, 2, 3).reshape(modes, cells)
-    entries = got[:, mode_dev:].reshape(owners, extra * cells)
-    entries = entries[:, : mode_dev * 2 * batches * nz].reshape(
-        owners, batches, per_batch, 2, batches, nz
-    )
-    entries = entries.transpose(3, 4, 1, 0, 2, 5).reshape(2, batches, modes, nz)
-    keys = entries[0].astype(jnp.int32)
-    places = jnp.arange(sources * kpad, dtype=jnp.int32)
-    dense = jnp.zeros((batches, modes, sources * kpad), jnp.float32)
-    for z in range(nz):
-        dense = dense + jnp.where(keys[:, :, z, None] == places, entries[1][:, :, z, None], 0.0)
-    dense = dense.reshape(batches, modes, sources, kpad).transpose(0, 2, 1, 3)
-    dense = dense.reshape(batches, sources * modes, kpad)
-
-    def window(x, margin):
-        padded = jnp.pad(x, ((0, 0), (0, 0), (margin, margin)))
-        return lax.dynamic_slice_in_dim(padded, me * cols, cols + 2 * margin, axis=2)
-
-    coef = halo_rows(window(coef_fields, depth), depth).reshape(fields, rows * width)
-    coef = jnp.pad(coef, ((0, kpad - fields), (0, cells - rows * width)))
-    mean = halo_rows(window(mean_field[None], depth + 1), depth + 1)[0]
-    mid = mean[1:-1, 1:-1]
-    diag = 0.5 * (
-        4.0 * mid + mean[2:, 1:-1] + mean[:-2, 1:-1] + mean[1:-1, 2:] + mean[1:-1, :-2]
-    )
-    row_ids = lax.axis_index("space") * slab - depth + jnp.arange(rows)
-    col_ids = me * cols - depth + jnp.arange(width)
-    total_rows = slab * lax.axis_size("space")
-    inside = ((row_ids >= 0) & (row_ids < total_rows))[:, None] & (
-        (col_ids >= 0) & (col_ids < ny)
-    )[None, :]
-    inv = jnp.where(inside, 1.0 / jnp.where(inside, diag, 1.0), 0.0).reshape(1, rows * width)
-    inv = jnp.pad(inv, ((0, 0), (0, cells - rows * width)))
-
-    patch = jax.ShapeDtypeStruct((modes, cells), jnp.float32)
+    both = jnp.stack([key, pair_value], axis=0).transpose(2, 0, 1, 3)
+    both = reorder(both.reshape(mode_dev, 2, batches * nz), pick)
+    both = jnp.pad(both, ((0, 0), (0, 0), (0, LANES - batches * nz)))
+    both = both.reshape(mode_dev, 2 * LANES)
+
+    side = jnp.pad(mean_field, ((0, 0), (1, 1)))
+    across = 4.0 * mean_field + side[:, 2:] + side[:, :-2]
+    later = jnp.pad(mean_field[1:], ((0, 1), (0, 0)))
+    before = jnp.pad(mean_field[:-1], ((1, 0), (0, 0)))
+    diag_parts = jnp.stack([across, mean_field, before, later], axis=0)
+    coef = jnp.concatenate([coef_fields, diag_parts], axis=0)
+    coef = jnp.pad(coef, ((0, kpad - fields - 4), (0, 0), (depth, depth)))
+    coef = lax.dynamic_slice_in_dim(coef, me * cols, width, axis=2).reshape(kpad, core_cells)
+
     vmem = pl.BlockSpec(memory_space=pltpu.VMEM)
     table = pltpu.VMEM((batches, sources * modes, cells), jnp.float32)
     state = pltpu.VMEM((modes, cells), jnp.float32)
     diff = pltpu.VMEM((sources, cells), jnp.float32)
-    coef6 = pltpu.VMEM((6 * kpad, cells), jnp.bfloat16)
-    sol, res = pl.pallas_call(
+    coef6 = pltpu.VMEM((8 * kpad, cells), jnp.bfloat16)
+    back = pl.pallas_call(
         functools.partial(sweep_kernel, dims),
-        out_shape=(patch, patch),
-        in_specs=[vmem] * 4,
-        out_specs=(vmem, vmem),
+        out_shape=jax.ShapeDtypeStruct((2, owners, mode_dev, core_cells), jnp.float32),
+        in_specs=[vmem] * 3,
+        out_specs=vmem,
         scratch_shapes=[
             table,
             table,
             state,
             state,
+            state,
+            state,
             diff,
             diff,
-            pltpu.VMEM((sources * modes, 6 * kpad), jnp.bfloat16),
+            pltpu.VMEM((sources * modes, 8 * kpad), jnp.bfloat16),
             coef6,
             coef6,
+            pltpu.VMEM((modes, 2 * LANES), jnp.float32),
+            pltpu.VMEM((kpad, cells), jnp.float32),
+            pltpu.VMEM((1, cells), jnp.float32),
+            pltpu.VMEM((sources * modes, 2 * LANES), jnp.float32),
+            pltpu.SemaphoreType.DMA((4, owners)),
+            pltpu.SemaphoreType.DMA((4, owners)),
+            pltpu.SemaphoreType.DMA((2, owners)),
+            pltpu.SemaphoreType.DMA((2, owners)),
+            pltpu.SemaphoreType.DMA((2,)),
+            pltpu.SemaphoreType.DMA((2,)),
         ],
-        compiler_params=pltpu.CompilerParams(vmem_limit_bytes=VMEM_BYTES),
+        compiler_params=pltpu.CompilerParams(
+            vmem_limit_bytes=VMEM_BYTES, collective_id=0, has_side_effects=True
+        ),
         name="sweeps",
-    )(values, coef, inv, dense)
-
-    done = jnp.stack([sol, res], axis=0)[:, :, : rows * width]
-    done = done.reshape(2, batches, owners, per_batch, rows, width)
-    done = done[..., depth : depth + slab, depth : depth + cols]
-    done = done.transpose(2, 0, 1, 3, 4, 5).reshape(owners, 2 * mode_dev * slab * cols)
-    back = lax.all_to_all(done, "mode", 0, 0, tiled=True)
-    back = back.reshape(owners, 2, mode_dev, slab, cols).transpose(2, 1, 3, 0, 4)
-    back = reorder(back.reshape(mode_dev, 2, slab, ny), pick.T)
+    )(win, both, coef)
+
+    back = back.reshape(2, owners, mode_dev, slab, width)[..., depth : depth + cols]
+    back = back.transpose(2, 0, 3, 1, 4).reshape(mode_dev, 2, slab, ny)
+    back = reorder(back, pick.T)
     return back[:, 0], back[:, 1]
 
 

time: 144 us -> 70.5 us (0.49)
  other arithmetic: 34.3 us -> 2.03 us
  Pallas kernels: 29.1 us -> 56.4 us
  starting transfers between devices: 21.4 us -> 0 us
  waiting for transfers between devices: 18.6 us -> 0 us
  local copies, waits for them, and re-layouts: 24.9 us -> 10.7 us
  blocking collectives: 13.5 us -> 0 us
    add x2 -> x1, other arithmetic: 28 us -> 0.01 us  [by_patch(): pool_rows = mode_ids // mode_dev * per_batch + ranking]
    pallas_call x1, Pallas kernels: 29.1 us -> 56.4 us  [by_patch(): pl.pallas_call(functools.partial(sweep_kernel, dims), out_shape=jax.Shape...]
    all_to_all x1 -> x0, waiting for transfers between devices: 18.5 us -> none  [by_patch(): got = lax.all_to_all(out, 'mode', 0, 0, tiled=True)]
    ppermute x6 -> x0, starting transfers between devices: 15.7 us -> none  [the longest x3 11.8 us: with_halo(): lax.ppermute(lax.slice_in_dim(block, block.shape[dim] - width, None, axis...]
    all_to_all x1 -> x0, blocking collectives: 13.5 us -> none  [by_patch(): back = lax.all_to_all(done, 'mode', 0, 0, tiled=True)]
    slice x11 -> x3, local copies, waits for them, and re-layouts: 7.13 us -> 0.55 us  [the longest x1 0.34 us: by_patch(): back.reshape(2, owners, mode_dev, slab, width)[..., depth:depth + cols]]
    all_to_all x1 -> x0, starting transfers between devices: 5.67 us -> none  [by_patch(): got = lax.all_to_all(out, 'mode', 0, 0, tiled=True)]
    another operation x13 -> x9, local copies, waits for them, and re-layouts: 4.31 us -> 0.72 us  [by_patch(): jnp.stack([padded[:, :, m * cols:m * cols + width] for m in range(owners)...]
  transfers between devices with their start and end apart: 7 -> 0, of which waited for: 1 -> 0; matrix products, arithmetic and copies ran while one was open for 9% -> 0% of each run, Pallas kernels for 0% -> 0%
where the time goes in v2:
time: 70.5 us; the launch traced here: 70 us
  Pallas kernels  56.4 us (80%)
  local copies, waits for them, and re-layouts  10.7 us (15%)
  other arithmetic  2.03 us (3%)
  between operations  0.89 us (1%)
    pallas_call x1, Pallas kernels, by_patch(): pl.pallas_call(functools.partial(sweep_kernel, dims), out_shape=jax.Shape...  56.4 us
    unnamed x27, local copies, waits for them, and re-layouts  3.78 us
    reshape x1, local copies, waits for them, and re-layouts, by_patch(): back.reshape(2, owners, mode_dev, slab, width)[..., depth:depth + cols]  1.54 us
    broadcast_in_dim x18, local copies, waits for them, and re-layouts, reorder(): jnp.where(table[:, j].reshape((-1,) + (1,) * (x.ndim - 1)), x[j][None], j...  1.44 us

profile of v2, /device:TPU:0, one launch (start us, length us, event | category | flops | bytes accessed | tf_op | source)
XLA Modules:
  0.0 70.0 jit_solution(123894748775556285)
XLA Ops:
  0.6 0.6 copy-done.7
  1.3 0.1 eq.49
  1.4 0.6 reduce_window_sum.11
  2.0 0.1 reshape.86
  2.1 0.1 dynamic_slice.6
  2.2 0.1 iota_compare_fusion.3
  2.3 0.7 %copy-done.5 = s32[4,8,24]{2,1,0:T(8,128)S(1)} copy-done((s32[4,8,24]{2,1,0:T(8,128)S(1)}, s32[4,8,24]{2,1,0:T(8,128)}, u32[]{:S(2)}) %copy-start.5) | copy-done | bytes 3096
  3.0 0.7 %select_reduce_fusion = s32[4,8,24]{2,1,0:T(8,128)S(1)} fusion(s32[64]{0:T(128)S(1)} %get-tuple-element.56, s32[4,8,24]{2,1,0:T(8,128)S(1)} %copy-done.5), kind=kLoop, calls=%fused_computation.2 | loop fusion | flops 146688 | bytes 6400 | tf_op jit(solution)/shard_map/reduce_sum | solution.py:387
  3.8 0.7 copy-done.6
  4.5 0.1 slice_reduce_fusion.7
  4.6 0.1 broadcast_in_dim.422
  4.7 0.1 broadcast_in_dim.444
  4.8 0.1 broadcast_in_dim.441
  4.9 0.1 broadcast_in_dim.438
  5.0 0.1 broadcast_in_dim.435
  5.0 0.1 broadcast_in_dim.432
  5.1 0.1 broadcast_in_dim.429
  5.2 0.1 broadcast_in_dim.426
  5.3 0.1 select_add_fusion.2
  5.4 0.6 pad_bitcast_fusion.pairs
  6.0 0.1 select_add_fusion.1
  6.2 0.2 pad_slice_fusion
  6.4 0.1 stack.55
  6.5 0.1 stack.54
  6.6 0.1 stack.53
  6.7 0.1 stack.52
  6.8 0.1 stack.51
  6.9 0.1 stack.50
  7.0 0.1 stack.49
  7.1 0.1 stack.48
  7.2 0.4 copy-done
  7.6 0.6 copy-done.2
  8.4 0.1 pad_dynamic-slice_fusion
  8.5 0.8 %reshape.88.cw = f32[32,768]{1,0:T(8,128)} reshape(f32[32,16,48]{2,1,0:T(8,128)S(1)} %pad_dynamic-slice_fusion) | data formatting | bytes 196608 | tf_op jit(solution)/shard_map/reshape | solution.py:419
  9.3 56.4 %sweeps.1 = f32[2,8,8,768]{3,2,1,0:T(8,128)} custom-call(f32[8,8,768]{2,1,0:T(8,128)} %copy-done.2, f32[8,256]{1,0:T(8,128)} %pad_bitcast_fusion.pairs, f32[32,768]{1,0:T(8,128)} %reshape.88.cw), custom_call_target="tpu_custom_call" | custom-call | tf_op jit(solution)/shard_map/sweeps/pallas_call | solution.py:426
  65.7 1.5 %reshape.89 = f32[2,8,8,16,48]{4,3,2,1,0:T(8,128)S(1)} reshape(f32[2,8,8,768]{3,2,1,0:T(8,128)} %sweeps.1) | data formatting | bytes 786432 | tf_op jit(solution)/shard_map/reshape | solution.py:460
  67.3 0.3 slice.264
  67.6 0.6 copy.13
  68.3 0.1 broadcast_in_dim.446
  68.4 0.1 broadcast_in_dim.475
  68.5 0.1 broadcast_in_dim.471
  68.6 0.1 broadcast_in_dim.467
  68.7 0.1 broadcast_in_dim.463
  68.8 0.1 broadcast_in_dim.459
  68.9 0.1 broadcast_in_dim.455
  69.0 0.1 broadcast_in_dim.451
  69.1 0.2 select_add_fusion
  69.3 0.7 %slice_bitcast_fusion = (f32[8,16,256]{2,1,0:T(8,128)}, f32[8,16,256]{2,1,0:T(8,128)}) fusion(f32[8,2,16,256]{3,2,0,1:T(8,128)S(1)} %select_add_fusion), kind=kLoop, calls=%fused_computation.7 | loop fusion | bytes 524288 | tf_op jit(solution)/shard_map/squeeze | solution.py:463
  (33 shorter events, 0.4 us)
Async XLA Ops:
  0.6 0.7 copy-start.7
  2.3 0.7 %copy-start.5 = (s32[4,8,24]{2,1,0:T(8,128)S(1)}, s32[4,8,24]{2,1,0:T(8,128)}, u32[]{:S(2)}) copy-start(s32[4,8,24]{2,1,0:T(8,128)} %param.11) | copy-start | bytes 9220
  3.0 0.8 %copy-start.4 = (s32[4,8,24]{2,1,0:T(8,128)S(1)}, s32[4,8,24]{2,1,0:T(8,128)}, u32[]{:S(2)}) copy-start(s32[4,8,24]{2,1,0:T(8,128)} %param.12) | copy-start | bytes 9220
  3.8 0.7 %copy-start.6 = (f32[4,8,24]{2,1,0:T(8,128)S(1)}, f32[4,8,24]{2,1,0:T(8,128)}, u32[]{:S(2)}) copy-start(f32[4,8,24]{2,1,0:T(8,128)} %param.13) | copy-start | bytes 9220
  4.5 1.5 %copy-start.3 = (f32[8,16,256]{2,1,0:T(8,128)S(1)}, f32[8,16,256]{2,1,0:T(8,128)}, u32[]{:S(2)}) copy-start(f32[8,16,256]{2,1,0:T(8,128)} %param.7) | copy-start | bytes 393220
  5.3 0.7 %copy-start.1 = (f32[16,256]{1,0:T(8,128)S(1)}, f32[16,256]{1,0:T(8,128)}, u32[]{:S(2)}) copy-start(f32[16,256]{1,0:T(8,128)} %param.8) | copy-start | bytes 49156
  6.6 1.0 %copy-start = (f32[28,16,256]{2,1,0:T(8,128)S(1)}, f32[28,16,256]{2,1,0:T(8,128)}, u32[]{:S(2)}) copy-start(f32[28,16,256]{2,1,0:T(8,128)} %param.9) | copy-start | bytes 1376260
  7.6 0.7 copy-start.2

commit v3 on v2

--- a/solution.py
+++ b/solution.py
@@ -116,7 +116,7 @@
 
 
 def sweep_kernel(dims, win, pairs, cw, back, ax, ay, r, sol, ex, ey, dvx, dvy, w6, a6x, a6y,
-                 allp, cbuf, inv, dense, send, recv, hsend, hrecv, csend, crecv):
+                 allp, cbuf, inv, dense, send, recv, hsend, hrecv, csend, crecv, packed):
     batches, sources, modes, width, steps, cells, rows, fields, nz, owners, slabs = dims
     mode_dev = modes // owners
     per_batch = mode_dev // batches
@@ -239,42 +239,48 @@
         pair_copy(d, me).wait_send()
         pair_copy(d, me).wait_recv()
 
-    chunk = 2 * LANES
+    chunk = 4 * LANES
     per_group = LANES // kpad
     lane = lax.broadcasted_iota(jnp.int32, (8, LANES), 1)
     lane_f = lane.astype(jnp.float32)
     value_lane = allp.shape[1] // 2
 
     def build(c):
-        @pl.loop(0, blocks)
-        def _(b):
-            own = allp[pl.ds(pl.multiple_of(b * 8, 8), 8), :]
-            sums = [jnp.zeros((8, LANES), jnp.float32)] * (sources // per_group)
-            for z in range(nz):
-                e = c * nz + z
-                key = jnp.broadcast_to(own[:, e : e + 1], (8, LANES))
-                val = jnp.broadcast_to(own[:, value_lane + e : value_lane + e + 1], (8, LANES))
-                for g in range(sources // per_group):
-                    sums[g] = sums[g] + jnp.where(key == lane_f + float(g * LANES), val, 0.0)
-            for g in range(sources // per_group):
-                for j in range(per_group):
-                    one = jnp.where((lane >= j * kpad) & (lane < (j + 1) * kpad), sums[g], 0.0)
-                    one = one + pltpu.roll(one, kpad, 1)
-                    one = one + pltpu.roll(one, 2 * kpad, 1)
-                    hi, mid, rest = split3(one)
-                    first = jnp.where(lane < 3 * kpad, hi, mid)
-                    second = jnp.where(lane < kpad, mid, jnp.where(lane < 2 * kpad, rest, 0.0))
-                    at = pl.ds(pl.multiple_of((g * per_group + j) * modes + b * 8, 8), 8)
-                    dense[at, pl.ds(0, LANES)] = first
-                    dense[at, pl.ds(LANES, LANES)] = second
+        @pl.loop(0, blocks // 2)
+        def _(pair):
+            build_rows(c, 2 * pair)
+            build_rows(c, 2 * pair + 1)
 
         w6[...] = dense[...].astype(jnp.bfloat16)
 
         @pl.loop(0, cells // chunk)
         def _(n):
             at = pl.ds(pl.multiple_of(n * chunk, chunk), chunk)
-            ax[c, :, at] = jnp.dot(w6[...], a6x[:, at], preferred_element_type=jnp.float32)
-            ay[c, :, at] = jnp.dot(w6[...], a6y[:, at], preferred_element_type=jnp.float32)
+            for table, a6 in ((ax, a6x), (ay, a6y)):
+                got = jnp.dot(w6[...], a6[:, at], preferred_element_type=jnp.float32)
+                for q in range(chunk // LANES):
+                    table[c, n * (chunk // LANES) + q] = got[:, q * LANES : (q + 1) * LANES]
+
+    def build_rows(c, b):
+        own = allp[pl.ds(pl.multiple_of(b * 8, 8), 8), :]
+        sums = [jnp.zeros((8, LANES), jnp.float32)] * (sources // per_group)
+        for z in range(nz):
+            e = c * nz + z
+            key = jnp.broadcast_to(own[:, e : e + 1], (8, LANES))
+            val = jnp.broadcast_to(own[:, value_lane + e : value_lane + e + 1], (8, LANES))
+            for g in range(sources // per_group):
+                sums[g] = sums[g] + jnp.where(key == lane_f + float(g * LANES), val, 0.0)
+        for g in range(sources // per_group):
+            for j in range(per_group):
+                one = jnp.where((lane >= j * kpad) & (lane < (j + 1) * kpad), sums[g], 0.0)
+                one = one + pltpu.roll(one, kpad, 1)
+                one = one + pltpu.roll(one, 2 * kpad, 1)
+                hi, mid, rest = split3(one)
+                first = jnp.where(lane < 3 * kpad, hi, mid)
+                second = jnp.where(lane < kpad, mid, jnp.where(lane < 2 * kpad, rest, 0.0))
+                at = pl.ds(pl.multiple_of((g * per_group + j) * modes + b * 8, 8), 8)
+                dense[at, pl.ds(0, LANES)] = first
+                dense[at, pl.ds(LANES, LANES)] = second
 
     build(0)
     for d in range(owners):
@@ -291,9 +297,22 @@
         pl.when(has_low)(lambda: up_copy(d, origin(d)).wait_recv())
         pl.when(has_high)(lambda: down_copy(d, origin(d)).wait_recv())
 
-    def out_copy(which, src, d):
+    cols = width - 2 * steps
+
+    def pack(which, src):
+        for b in range(blocks):
+            x = src[pl.ds(b * 8, 8), mid_at]
+            packed[which, pl.ds(b * 8, 8), :] = jnp.concatenate(
+                [
+                    x[:, q * width + steps : q * width + steps + cols]
+                    for q in range(core_cells // width)
+                ],
+                axis=1,
+            )
+
+    def out_copy(which, d):
         return remote(
-            src.at[owner_rows(peer(d)), mid_at], back.at[which, me], send.at[2 + which, d],
+            packed.at[which, owner_rows(peer(d))], back.at[which, me], send.at[2 + which, d],
             recv.at[2 + which, d], mode=peer(d),
         )
 
@@ -309,8 +328,9 @@
         dvx[...] = u - pltpu.roll(u, cells - width, 1)
         dvy[...] = u - pltpu.roll(u, cells - 1, 1)
         if k == steps - 1:
+            pack(0, sol)
             for d in range(1, owners):
-                out_copy(0, sol, d).start()
+                out_copy(0, d).start()
         first = (width * k) // LANES
         last = -(-(width * (rows - 1 - k)) // LANES)
 
@@ -322,7 +342,7 @@
                 for s in range(sources):
                     dv = jnp.broadcast_to(diff[pl.ds(s, 1), at], (8, LANES))
                     for b in range(blocks):
-                        term = table[c, pl.ds(s * modes + b * 8, 8), at] * dv
+                        term = table[c, g, pl.ds(s * modes + b * 8, 8), :] * dv
                         sums[b] = term if s == 0 else sums[b] + term
                 for b in range(blocks):
                     out[pl.ds(b * 8, 8), at] = sums[b]
@@ -334,14 +354,15 @@
             div = (x - pltpu.roll(x, width, 1)) + (y - pltpu.roll(y, 1, 1))
             r[some, :] = r[some, :] - div
 
+    pack(1, r)
     for d in range(1, owners):
-        out_copy(1, r, d).start()
-    for which, src in ((0, sol), (1, r)):
-        back[which, me] = src[owner_rows(me), mid_at]
-    for which, src in ((0, sol), (1, r)):
+        out_copy(1, d).start()
+    for which in range(2):
+        back[which, me] = packed[which, owner_rows(me), :]
+    for which in range(2):
         for d in range(1, owners):
-            out_copy(which, src, d).wait_send()
-            out_copy(which, src, d).wait_recv()
+            out_copy(which, d).wait_send()
+            out_copy(which, d).wait_recv()
 
 
 def patch_sizes(mesh, forcing, pair_src, coef_fields):
@@ -362,7 +383,8 @@
     fits = (
         table + 12_000_000 < VMEM_BYTES
         and slab > depth
-        and cells % (2 * LANES) == 0
+        and cells % (4 * LANES) == 0
+        and (slab * cols) % LANES == 0
         and (width * depth) % LANES == 0
         and modes == 8 * owners
         and sources % 8 == 0
@@ -419,13 +441,13 @@
     coef = lax.dynamic_slice_in_dim(coef, me * cols, width, axis=2).reshape(kpad, core_cells)
 
     vmem = pl.BlockSpec(memory_space=pltpu.VMEM)
-    table = pltpu.VMEM((batches, sources * modes, cells), jnp.float32)
+    table = pltpu.VMEM((batches, cells // LANES, sources * modes, LANES), jnp.float32)
     state = pltpu.VMEM((modes, cells), jnp.float32)
     diff = pltpu.VMEM((sources, cells), jnp.float32)
     coef6 = pltpu.VMEM((8 * kpad, cells), jnp.bfloat16)
     back = pl.pallas_call(
         functools.partial(sweep_kernel, dims),
-        out_shape=jax.ShapeDtypeStruct((2, owners, mode_dev, core_cells), jnp.float32),
+        out_shape=jax.ShapeDtypeStruct((2, owners, mode_dev, slab * cols), jnp.float32),
         in_specs=[vmem] * 3,
         out_specs=vmem,
         scratch_shapes=[
@@ -450,6 +472,7 @@
             pltpu.SemaphoreType.DMA((2, owners)),
             pltpu.SemaphoreType.DMA((2,)),
             pltpu.SemaphoreType.DMA((2,)),
+            pltpu.VMEM((2, modes, slab * cols), jnp.float32),
         ],
         compiler_params=pltpu.CompilerParams(
             vmem_limit_bytes=VMEM_BYTES, collective_id=0, has_side_effects=True
@@ -457,7 +480,7 @@
         name="sweeps",
     )(win, both, coef)
 
-    back = back.reshape(2, owners, mode_dev, slab, width)[..., depth : depth + cols]
+    back = back.reshape(2, owners, mode_dev, slab, cols)
     back = back.transpose(2, 0, 3, 1, 4).reshape(mode_dev, 2, slab, ny)
     back = reorder(back, pick.T)
     return back[:, 0], back[:, 1]

time: 70.5 us -> 58.7 us (0.83)
  Pallas kernels: 56.4 us -> 45.2 us
    pallas_call x1, Pallas kernels: 56.4 us -> 45.2 us  [by_patch(): pl.pallas_call(functools.partial(sweep_kernel, dims), out_shape=jax.Shape...]
    unnamed x27 -> x26, local copies, waits for them, and re-layouts: 3.78 us -> 3.18 us
    reshape x1 -> x2, local copies, waits for them, and re-layouts: 1.54 us -> 1.83 us  [by_patch(): back = back.reshape(2, owners, mode_dev, slab, cols)]
where the time goes in v3:
time: 58.7 us; the launch traced here: 58.1 us
  Pallas kernels  45.2 us (77%)
  local copies, waits for them, and re-layouts  10.1 us (17%)
  other arithmetic  2.03 us (3%)
  between operations  0.89 us (2%)
    pallas_call x1, Pallas kernels, by_patch(): pl.pallas_call(functools.partial(sweep_kernel, dims), out_shape=jax.Shape...  45.2 us
    unnamed x26, local copies, waits for them, and re-layouts  3.18 us
    reshape x2, local copies, waits for them, and re-layouts, by_patch(): back = back.reshape(2, owners, mode_dev, slab, cols)  1.83 us
    broadcast_in_dim x18, local copies, waits for them, and re-layouts, reorder(): jnp.where(table[:, j].reshape((-1,) + (1,) * (x.ndim - 1)), x[j][None], j...  1.44 us

profile of v3, /device:TPU:0, one launch (start us, length us, event | category | flops | bytes accessed | tf_op | source)
XLA Modules:
  0.0 58.1 jit_solution(1397094427853806453)
XLA Ops:
  0.6 0.6 %copy-done.7 = s32[64]{0:T(128)S(1)} copy-done((s32[64]{0:T(128)S(1)}, s32[64]{0:T(128)}, u32[]{:S(2)}) %copy-start.7) | copy-done | bytes 280
  1.3 0.1 eq.49
  1.4 0.6 %reduce_window_sum.11 = s32[8,8,4]{1,0,2:T(8,128)S(1)} reduce-window(s32[8,8,4]{1,0,2:T(8,128)S(1)} %fusion.3, s32[]{:T(128)} %constant.31.clone.1), window={size=1x8x1 pad=0_0x7_0x0_0}, to_apply=%region_0.0 | reduce-window | flops 1792 | bytes 2052 | tf_op jit(solution)/shard_map/jit(cumsum)/reduce_window_sum | solution.py:68
  2.0 0.1 reshape.86
  2.1 0.1 dynamic_slice.6
  2.2 0.1 iota_compare_fusion.3
  2.3 0.7 %copy-done.5 = s32[4,8,24]{2,1,0:T(8,128)S(1)} copy-done((s32[4,8,24]{2,1,0:T(8,128)S(1)}, s32[4,8,24]{2,1,0:T(8,128)}, u32[]{:S(2)}) %copy-start.5) | copy-done | bytes 3096
  3.0 0.7 %select_reduce_fusion = s32[4,8,24]{2,1,0:T(8,128)S(1)} fusion(s32[64]{0:T(128)S(1)} %get-tuple-element.56, s32[4,8,24]{2,1,0:T(8,128)S(1)} %copy-done.5), kind=kLoop, calls=%fused_computation.2 | loop fusion | flops 146688 | bytes 6400 | tf_op jit(solution)/shard_map/reduce_sum | solution.py:409
  3.8 0.7 %copy-done.6 = f32[4,8,24]{2,1,0:T(8,128)S(1)} copy-done((f32[4,8,24]{2,1,0:T(8,128)S(1)}, f32[4,8,24]{2,1,0:T(8,128)}, u32[]{:S(2)}) %copy-start.6) | copy-done | bytes 3096
  4.5 0.1 slice_reduce_fusion.7
  4.6 0.1 broadcast_in_dim.422
  4.7 0.1 broadcast_in_dim.444
  4.8 0.1 broadcast_in_dim.441
  4.9 0.1 broadcast_in_dim.438
  5.0 0.1 broadcast_in_dim.435
  5.0 0.1 broadcast_in_dim.432
  5.1 0.1 broadcast_in_dim.429
  5.2 0.1 broadcast_in_dim.426
  5.3 0.1 select_add_fusion.2
  5.4 0.6 %pad_bitcast_fusion.pairs = f32[8,256]{1,0:T(8,128)} fusion(f32[8,2,96]{2,0,1:T(8,128)S(1)} %select_add_fusion.2), kind=kLoop, calls=%fused_computation.41 | loop fusion | bytes 14336 | tf_op jit(solution)/shard_map/reshape | solution.py:432
  6.0 0.1 select_add_fusion.1
  6.2 0.2 pad_slice_fusion
  6.4 0.1 stack.55
  6.5 0.1 stack.54
  6.6 0.1 stack.53
  6.7 0.1 stack.52
  6.8 0.1 stack.51
  6.9 0.1 stack.50
  7.0 0.1 stack.49
  7.1 0.1 stack.48
  7.2 0.4 copy-done
  7.6 0.6 %copy-done.2 = f32[8,8,768]{2,1,0:T(8,128)} copy-done((f32[8,8,768]{2,1,0:T(8,128)}, f32[8,8,768]{2,1,0:T(8,128)S(1)}, u32[]{:S(2)}) %copy-start.2) | copy-done | bytes 196632
  8.3 0.1 constant_dynamic-update-slice_fusion.11
  8.4 0.1 pad_dynamic-slice_fusion
  8.5 0.8 %reshape.88.cw = f32[32,768]{1,0:T(8,128)} reshape(f32[32,16,48]{2,1,0:T(8,128)S(1)} %pad_dynamic-slice_fusion) | data formatting | bytes 196608 | tf_op jit(solution)/shard_map/reshape | solution.py:441
  9.3 45.2 %sweeps.1 = f32[2,8,8,512]{3,2,1,0:T(8,128)} custom-call(f32[8,8,768]{2,1,0:T(8,128)} %copy-done.2, f32[8,256]{1,0:T(8,128)} %pad_bitcast_fusion.pairs, f32[32,768]{1,0:T(8,128)} %reshape.88.cw), custom_call_target="tpu_custom_call" | custom-call | tf_op jit(solution)/shard_map/sweeps/pallas_call | solution.py:448
  54.5 1.2 %reshape.89 = f32[2,8,8,16,32]{4,3,2,1,0:T(8,128)S(1)} reshape(f32[2,8,8,512]{3,2,1,0:T(8,128)} %sweeps.1) | data formatting | bytes 524288 | tf_op jit(solution)/shard_map/reshape | solution.py:483
  55.7 0.6 %copy.12 = f32[2,8,8,16,32]{4,1,3,0,2:T(8,128)S(1)} copy(f32[2,8,8,16,32]{4,3,2,1,0:T(8,128)S(1)} %reshape.89) | data formatting | bytes 524288 | tf_op jit(solution)/shard_map/reshape | solution.py:483
  56.4 0.1 broadcast_in_dim.446
  56.5 0.1 broadcast_in_dim.475
  56.6 0.1 broadcast_in_dim.471
  56.7 0.1 broadcast_in_dim.467
  56.8 0.1 broadcast_in_dim.463
  56.9 0.1 broadcast_in_dim.459
  57.0 0.1 broadcast_in_dim.455
  57.1 0.1 broadcast_in_dim.451
  57.2 0.2 select_add_fusion
  57.4 0.7 %slice_bitcast_fusion = (f32[8,16,256]{2,1,0:T(8,128)}, f32[8,16,256]{2,1,0:T(8,128)}) fusion(f32[8,2,16,256]{3,2,0,1:T(8,128)S(1)} %select_add_fusion), kind=kLoop, calls=%fused_computation.7 | loop fusion | bytes 524288 | tf_op jit(solution)/shard_map/squeeze | solution.py:486
  (32 shorter events, 0.3 us)
Async XLA Ops:
  0.6 0.7 %copy-start.7 = (s32[64]{0:T(128)S(1)}, s32[64]{0:T(128)}, u32[]{:S(2)}) copy-start(s32[64]{0:T(128)} %param.10) | copy-start | bytes 772
  2.3 0.7 %copy-start.5 = (s32[4,8,24]{2,1,0:T(8,128)S(1)}, s32[4,8,24]{2,1,0:T(8,128)}, u32[]{:S(2)}) copy-start(s32[4,8,24]{2,1,0:T(8,128)} %param.11) | copy-start | bytes 9220
  3.0 0.8 %copy-start.4 = (s32[4,8,24]{2,1,0:T(8,128)S(1)}, s32[4,8,24]{2,1,0:T(8,128)}, u32[]{:S(2)}) copy-start(s32[4,8,24]{2,1,0:T(8,128)} %param.12) | copy-start | bytes 9220
  3.8 0.7 %copy-start.6 = (f32[4,8,24]{2,1,0:T(8,128)S(1)}, f32[4,8,24]{2,1,0:T(8,128)}, u32[]{:S(2)}) copy-start(f32[4,8,24]{2,1,0:T(8,128)} %param.13) | copy-start | bytes 9220
  4.5 1.5 %copy-start.3 = (f32[8,16,256]{2,1,0:T(8,128)S(1)}, f32[8,16,256]{2,1,0:T(8,128)}, u32[]{:S(2)}) copy-start(f32[8,16,256]{2,1,0:T(8,128)} %param.7) | copy-start | bytes 393220
  5.3 0.7 %copy-start.1 = (f32[16,256]{1,0:T(8,128)S(1)}, f32[16,256]{1,0:T(8,128)}, u32[]{:S(2)}) copy-start(f32[16,256]{1,0:T(8,128)} %param.8) | copy-start | bytes 49156
  6.6 1.0 %copy-start = (f32[28,16,256]{2,1,0:T(8,128)S(1)}, f32[28,16,256]{2,1,0:T(8,128)}, u32[]{:S(2)}) copy-start(f32[28,16,256]{2,1,0:T(8,128)} %param.9) | copy-start | bytes 1376260
  7.6 0.7 %copy-start.2 = (f32[8,8,768]{2,1,0:T(8,128)}, f32[8,8,768]{2,1,0:T(8,128)S(1)}, u32[]{:S(2)}) copy-start(f32[8,8,768]{2,1,0:T(8,128)S(1)} %constant_dynamic-update-slice_fusion.win) | copy-start | bytes 589828

commit v4 on v3

--- a/solution.py
+++ b/solution.py
@@ -151,9 +151,6 @@
                 barrier, inc=1, device_id={"space": at}, device_id_type=pl.DeviceIdType.MESH
             )
 
-    beside = has_low.astype(jnp.int32) + has_high.astype(jnp.int32)
-    pl.semaphore_wait(barrier, owners - 1 + beside)
-
     def peer(d):
         return lax.rem(me + d, owners)
 
@@ -192,74 +189,12 @@
             cw.at[:, pl.ds(0, edge)], cbuf.at[:, high], csend.at[1], crecv.at[1], space=slab - 1
         )
 
-    for d in range(1, owners):
-        pair_copy(d, me).start()
-    pl.when(has_high)(lambda: coef_up().start())
-    pl.when(has_low)(lambda: coef_down().start())
-    for d in range(1, owners):
-        value_copy(d, me).start()
-
-    allp[owner_rows(me), :] = pairs[...]
-    r[owner_rows(me), mid_at] = win[me]
-    cbuf[:, mid_at] = cw[...]
-    for there, at in ((has_low, low), (has_high, high)):
-
-        @pl.when(jnp.logical_not(there))
-        def _():
-            r[:, at] = jnp.zeros((modes, edge), jnp.float32)
-            cbuf[:, at] = jnp.zeros((cbuf.shape[0], edge), jnp.float32)
-
-    sol[...] = jnp.zeros_like(sol)
-    ex[...] = jnp.zeros_like(ex)
-    ey[...] = jnp.zeros_like(ey)
-
-    pl.when(has_high)(lambda: coef_up().wait_send())
-    pl.when(has_low)(lambda: coef_down().wait_send())
-    pl.when(has_low)(lambda: coef_up().wait_recv())
-    pl.when(has_high)(lambda: coef_down().wait_recv())
-    a = cbuf[...]
-    kpad = a.shape[0]
-    for a6, shift in ((a6x, width), (a6y, 1)):
-        parts = split3(0.5 * (a + pltpu.roll(a, cells - shift, 1)))
-        hi, mid, rest = [x.astype(jnp.bfloat16) for x in parts]
-        none = jnp.zeros_like(hi)
-        a6[...] = jnp.concatenate([hi, mid, rest, hi, mid, hi, none, none], axis=0)
-    extra = a[fields : fields + 4]
-    place = lax.broadcasted_iota(jnp.int32, (1, cells), 1)
-    centre, across = extra[1:2], extra[0:1]
-    above = jnp.where(place < width, extra[2:3], pltpu.roll(centre, width, 1))
-    below = jnp.where(
-        place >= width * (rows - 1), extra[3:4], pltpu.roll(centre, cells - width, 1)
-    )
-    inside = across > 0.0
-    diag = jnp.where(inside, 0.5 * (across + above + below), 1.0)
-    inv[...] = jnp.where(inside, 1.0 / diag, 0.0)
-
-    for d in range(1, owners):
-        pair_copy(d, me).wait_send()
-        pair_copy(d, me).wait_recv()
-
     chunk = 4 * LANES
+    kpad = cw.shape[0]
     per_group = LANES // kpad
     lane = lax.broadcasted_iota(jnp.int32, (8, LANES), 1)
     lane_f = lane.astype(jnp.float32)
     value_lane = allp.shape[1] // 2
-
-    def build(c):
-        @pl.loop(0, blocks // 2)
-        def _(pair):
-            build_rows(c, 2 * pair)
-            build_rows(c, 2 * pair + 1)
-
-        w6[...] = dense[...].astype(jnp.bfloat16)
-
-        @pl.loop(0, cells // chunk)
-        def _(n):
-            at = pl.ds(pl.multiple_of(n * chunk, chunk), chunk)
-            for table, a6 in ((ax, a6x), (ay, a6y)):
-                got = jnp.dot(w6[...], a6[:, at], preferred_element_type=jnp.float32)
-                for q in range(chunk // LANES):
-                    table[c, n * (chunk // LANES) + q] = got[:, q * LANES : (q + 1) * LANES]
 
     def build_rows(c, b):
         own = allp[pl.ds(pl.multiple_of(b * 8, 8), 8), :]
@@ -279,8 +214,73 @@
                 first = jnp.where(lane < 3 * kpad, hi, mid)
                 second = jnp.where(lane < kpad, mid, jnp.where(lane < 2 * kpad, rest, 0.0))
                 at = pl.ds(pl.multiple_of((g * per_group + j) * modes + b * 8, 8), 8)
-                dense[at, pl.ds(0, LANES)] = first
-                dense[at, pl.ds(LANES, LANES)] = second
+                dense[c, at, pl.ds(0, LANES)] = first
+                dense[c, at, pl.ds(LANES, LANES)] = second
+
+    allp[owner_rows(me), :] = pairs[...]
+    r[owner_rows(me), mid_at] = win[me]
+    cbuf[:, mid_at] = cw[...]
+    for there, at in ((has_low, low), (has_high, high)):
+
+        @pl.when(jnp.logical_not(there))
+        def _():
+            r[:, at] = jnp.zeros((modes, edge), jnp.float32)
+            cbuf[:, at] = jnp.zeros((cbuf.shape[0], edge), jnp.float32)
+
+    sol[...] = jnp.zeros_like(sol)
+    ex[...] = jnp.zeros_like(ex)
+    ey[...] = jnp.zeros_like(ey)
+
+    for c in range(batches):
+        build_rows(c, me)
+    beside = has_low.astype(jnp.int32) + has_high.astype(jnp.int32)
+    pl.semaphore_wait(barrier, owners - 1 + beside)
+
+    for d in range(1, owners):
+        pair_copy(d, me).start()
+    pl.when(has_high)(lambda: coef_up().start())
+    pl.when(has_low)(lambda: coef_down().start())
+    for d in range(1, owners):
+        value_copy(d, me).start()
+
+    @pl.loop(1, owners)
+    def _(d):
+        pair_copy(d, me).wait_send()
+        pair_copy(d, me).wait_recv()
+        for c in range(batches):
+            build_rows(c, origin(d))
+
+    pl.when(has_high)(lambda: coef_up().wait_send())
+    pl.when(has_low)(lambda: coef_down().wait_send())
+    pl.when(has_low)(lambda: coef_up().wait_recv())
+    pl.when(has_high)(lambda: coef_down().wait_recv())
+    a = cbuf[...]
+    for a6, shift in ((a6x, width), (a6y, 1)):
+        parts = split3(0.5 * (a + pltpu.roll(a, cells - shift, 1)))
+        hi, mid, rest = [x.astype(jnp.bfloat16) for x in parts]
+        none = jnp.zeros_like(hi)
+        a6[...] = jnp.concatenate([hi, mid, rest, hi, mid, hi, none, none], axis=0)
+    extra = a[fields : fields + 4]
+    place = lax.broadcasted_iota(jnp.int32, (1, cells), 1)
+    centre, across = extra[1:2], extra[0:1]
+    above = jnp.where(place < width, extra[2:3], pltpu.roll(centre, width, 1))
+    below = jnp.where(
+        place >= width * (rows - 1), extra[3:4], pltpu.roll(centre, cells - width, 1)
+    )
+    inside = across > 0.0
+    diag = jnp.where(inside, 0.5 * (across + above + below), 1.0)
+    inv[...] = jnp.where(inside, 1.0 / diag, 0.0)
+
+    def build(c):
+        w6[...] = dense[c].astype(jnp.bfloat16)
+
+        @pl.loop(0, cells // chunk)
+        def _(n):
+            at = pl.ds(pl.multiple_of(n * chunk, chunk), chunk)
+            for table, a6 in ((ax, a6x), (ay, a6y)):
+                got = jnp.dot(w6[...], a6[:, at], preferred_element_type=jnp.float32)
+                for q in range(chunk // LANES):
+                    table[c, n * (chunk // LANES) + q] = got[:, q * LANES : (q + 1) * LANES]
 
     build(0)
     for d in range(owners):
@@ -349,10 +349,11 @@
 
         for b in range(blocks):
             some = pl.ds(b * 8, 8)
-            x = ex[some, :]
-            y = ey[some, :]
+            span = pl.ds(first * LANES, (last - first) * LANES)
+            x = ex[some, span]
+            y = ey[some, span]
             div = (x - pltpu.roll(x, width, 1)) + (y - pltpu.roll(y, 1, 1))
-            r[some, :] = r[some, :] - div
+            r[some, span] = r[some, span] - div
 
     pack(1, r)
     for d in range(1, owners):
@@ -403,7 +404,10 @@
     kpad = LANES // 4
     core_cells = slab * width
     me = lax.axis_index("mode")
-    ranking = ranks(color, mode_dev, batches)
+    grouped = color.reshape(-1, mode_dev)
+    ahead = jnp.arange(mode_dev)[None, :] < jnp.arange(mode_dev)[:, None]
+    same = (grouped[:, :, None] == grouped[:, None, :]) & ahead[None]
+    ranking = jnp.sum(same.astype(jnp.int32), axis=2).reshape(-1)
     mode_ids = jnp.arange(modes, dtype=jnp.int32)
     pool_rows = (mode_ids // mode_dev) * per_batch + ranking
     source_rows = jnp.sum(
@@ -465,7 +469,7 @@
             pltpu.VMEM((modes, 2 * LANES), jnp.float32),
             pltpu.VMEM((kpad, cells), jnp.float32),
             pltpu.VMEM((1, cells), jnp.float32),
-            pltpu.VMEM((sources * modes, 2 * LANES), jnp.float32),
+            pltpu.VMEM((batches, sources * modes, 2 * LANES), jnp.float32),
             pltpu.SemaphoreType.DMA((4, owners)),
             pltpu.SemaphoreType.DMA((4, owners)),
             pltpu.SemaphoreType.DMA((2, owners)),

time: 58.7 us -> 54.3 us (0.925)
  Pallas kernels: 45.2 us -> 41.2 us
    pallas_call x1, Pallas kernels: 45.2 us -> 41.2 us  [by_patch(): pl.pallas_call(functools.partial(sweep_kernel, dims), out_shape=jax.Shape...]
    another operation x1 -> x0, other arithmetic: 0.65 us -> none  [ranks(): earlier = jnp.cumsum(onehot, axis=1) - onehot]
where the time goes in v4:
time: 54.3 us; the launch traced here: 53.8 us
  Pallas kernels  41.2 us (76%)
  local copies, waits for them, and re-layouts  10 us (18%)
  other arithmetic  1.66 us (3%)
  between operations  0.9 us (2%)
    pallas_call x1, Pallas kernels, by_patch(): pl.pallas_call(functools.partial(sweep_kernel, dims), out_shape=jax.Shape...  41.2 us
    unnamed x26, local copies, waits for them, and re-layouts  3.17 us
    reshape x2, local copies, waits for them, and re-layouts, by_patch(): back = back.reshape(2, owners, mode_dev, slab, cols)  1.83 us
    broadcast_in_dim x18, local copies, waits for them, and re-layouts, reorder(): jnp.where(table[:, j].reshape((-1,) + (1,) * (x.ndim - 1)), x[j][None], j...  1.44 us

profile of v4, /device:TPU:0, one launch (start us, length us, event | category | flops | bytes accessed | tf_op | source)
XLA Modules:
  0.0 53.8 jit_solution(242594060084787026)
XLA Ops:
  0.7 0.6 %copy-done.7 = s32[64]{0:T(128)S(1)} copy-done((s32[64]{0:T(128)S(1)}, s32[64]{0:T(128)}, u32[]{:S(2)}) %copy-start.7) | copy-done | bytes 280
  1.3 0.1 eq.51
  1.4 0.3 convert_reduce_fusion
  1.7 0.1 reshape.99
  1.8 0.1 dynamic_slice.6
  1.8 0.1 iota_compare_fusion.3
  1.9 0.7 %copy-done.5 = s32[4,8,24]{2,1,0:T(8,128)S(1)} copy-done((s32[4,8,24]{2,1,0:T(8,128)S(1)}, s32[4,8,24]{2,1,0:T(8,128)}, u32[]{:S(2)}) %copy-start.5) | copy-done | bytes 3096
  2.7 0.7 %select_reduce_fusion = s32[4,8,24]{2,1,0:T(8,128)S(1)} fusion(s32[64]{0:T(128)S(1)} %get-tuple-element.56, s32[4,8,24]{2,1,0:T(8,128)S(1)} %copy-done.5), kind=kLoop, calls=%fused_computation.2 | loop fusion | flops 146688 | bytes 6400 | tf_op jit(solution)/shard_map/reduce_sum | solution.py:413
  3.4 0.7 %copy-done.6 = f32[4,8,24]{2,1,0:T(8,128)S(1)} copy-done((f32[4,8,24]{2,1,0:T(8,128)S(1)}, f32[4,8,24]{2,1,0:T(8,128)}, u32[]{:S(2)}) %copy-start.6) | copy-done | bytes 3096
  4.1 0.1 slice_reduce_fusion.7
  4.3 0.1 broadcast_in_dim.424
  4.3 0.1 broadcast_in_dim.446
  4.4 0.1 broadcast_in_dim.443
  4.5 0.1 broadcast_in_dim.440
  4.6 0.1 broadcast_in_dim.437
  4.7 0.1 broadcast_in_dim.434
  4.8 0.1 broadcast_in_dim.431
  4.8 0.1 broadcast_in_dim.428
  4.9 0.1 select_add_fusion.2
  5.0 0.6 %pad_bitcast_fusion.pairs = f32[8,256]{1,0:T(8,128)} fusion(f32[8,2,96]{2,0,1:T(8,128)S(1)} %select_add_fusion.2), kind=kLoop, calls=%fused_computation.39 | loop fusion | bytes 14336 | tf_op jit(solution)/shard_map/reshape | solution.py:436
  5.7 0.1 select_add_fusion.1
  5.8 0.2 pad_slice_fusion
  6.0 0.1 stack.55
  6.1 0.1 stack.54
  6.2 0.1 stack.53
  6.3 0.1 stack.52
  6.4 0.1 stack.51
  6.5 0.1 stack.50
  6.6 0.1 stack.49
  6.7 0.1 stack.48
  6.9 0.4 copy-done
  7.3 0.6 %copy-done.2 = f32[8,8,768]{2,1,0:T(8,128)} copy-done((f32[8,8,768]{2,1,0:T(8,128)}, f32[8,8,768]{2,1,0:T(8,128)S(1)}, u32[]{:S(2)}) %copy-start.2) | copy-done | bytes 196632
  7.9 0.1 constant_dynamic-update-slice_fusion.11
  8.0 0.1 pad_dynamic-slice_fusion
  8.2 0.8 %reshape.101.cw = f32[32,768]{1,0:T(8,128)} reshape(f32[32,16,48]{2,1,0:T(8,128)S(1)} %pad_dynamic-slice_fusion) | data formatting | bytes 196608 | tf_op jit(solution)/shard_map/reshape | solution.py:445
  9.0 41.2 %sweeps.1 = f32[2,8,8,512]{3,2,1,0:T(8,128)} custom-call(f32[8,8,768]{2,1,0:T(8,128)} %copy-done.2, f32[8,256]{1,0:T(8,128)} %pad_bitcast_fusion.pairs, f32[32,768]{1,0:T(8,128)} %reshape.101.cw), custom_call_target="tpu_custom_call" | custom-call | tf_op jit(solution)/shard_map/sweeps/pallas_call | solution.py:452
  50.2 1.2 %reshape.102 = f32[2,8,8,16,32]{4,3,2,1,0:T(8,128)S(1)} reshape(f32[2,8,8,512]{3,2,1,0:T(8,128)} %sweeps.1) | data formatting | bytes 524288 | tf_op jit(solution)/shard_map/reshape | solution.py:487
  51.4 0.6 %copy.12 = f32[2,8,8,16,32]{4,1,3,0,2:T(8,128)S(1)} copy(f32[2,8,8,16,32]{4,3,2,1,0:T(8,128)S(1)} %reshape.102) | data formatting | bytes 524288 | tf_op jit(solution)/shard_map/reshape | solution.py:487
  52.1 0.1 broadcast_in_dim.448
  52.2 0.1 broadcast_in_dim.477
  52.3 0.1 broadcast_in_dim.473
  52.4 0.1 broadcast_in_dim.469
  52.5 0.1 broadcast_in_dim.465
  52.6 0.1 broadcast_in_dim.461
  52.7 0.1 broadcast_in_dim.457
  52.8 0.1 broadcast_in_dim.453
  52.9 0.2 select_add_fusion
  53.1 0.7 %slice_bitcast_fusion = (f32[8,16,256]{2,1,0:T(8,128)}, f32[8,16,256]{2,1,0:T(8,128)}) fusion(f32[8,2,16,256]{3,2,0,1:T(8,128)S(1)} %select_add_fusion), kind=kLoop, calls=%fused_computation.7 | loop fusion | bytes 524288 | tf_op jit(solution)/shard_map/squeeze | solution.py:490
  (31 shorter events, 0.3 us)
Async XLA Ops:
  0.6 0.7 %copy-start.7 = (s32[64]{0:T(128)S(1)}, s32[64]{0:T(128)}, u32[]{:S(2)}) copy-start(s32[64]{0:T(128)} %param.10) | copy-start | bytes 772
  1.9 0.7 %copy-start.5 = (s32[4,8,24]{2,1,0:T(8,128)S(1)}, s32[4,8,24]{2,1,0:T(8,128)}, u32[]{:S(2)}) copy-start(s32[4,8,24]{2,1,0:T(8,128)} %param.11) | copy-start | bytes 9220
  2.6 0.8 %copy-start.4 = (s32[4,8,24]{2,1,0:T(8,128)S(1)}, s32[4,8,24]{2,1,0:T(8,128)}, u32[]{:S(2)}) copy-start(s32[4,8,24]{2,1,0:T(8,128)} %param.12) | copy-start | bytes 9220
  3.4 0.7 %copy-start.6 = (f32[4,8,24]{2,1,0:T(8,128)S(1)}, f32[4,8,24]{2,1,0:T(8,128)}, u32[]{:S(2)}) copy-start(f32[4,8,24]{2,1,0:T(8,128)} %param.13) | copy-start | bytes 9220
  4.1 1.5 %copy-start.3 = (f32[8,16,256]{2,1,0:T(8,128)S(1)}, f32[8,16,256]{2,1,0:T(8,128)}, u32[]{:S(2)}) copy-start(f32[8,16,256]{2,1,0:T(8,128)} %param.7) | copy-start | bytes 393220
  4.9 0.7 %copy-start.1 = (f32[16,256]{1,0:T(8,128)S(1)}, f32[16,256]{1,0:T(8,128)}, u32[]{:S(2)}) copy-start(f32[16,256]{1,0:T(8,128)} %param.8) | copy-start | bytes 49156
  6.2 1.0 %copy-start = (f32[28,16,256]{2,1,0:T(8,128)S(1)}, f32[28,16,256]{2,1,0:T(8,128)}, u32[]{:S(2)}) copy-start(f32[28,16,256]{2,1,0:T(8,128)} %param.9) | copy-start | bytes 1376260
  7.2 0.7 %copy-start.2 = (f32[8,8,768]{2,1,0:T(8,128)}, f32[8,8,768]{2,1,0:T(8,128)S(1)}, u32[]{:S(2)}) copy-start(f32[8,8,768]{2,1,0:T(8,128)S(1)} %constant_dynamic-update-slice_fusion.win) | copy-start | bytes 589828

commit v5 on v4

--- a/solution.py
+++ b/solution.py
@@ -189,7 +189,9 @@
             cw.at[:, pl.ds(0, edge)], cbuf.at[:, high], csend.at[1], crecv.at[1], space=slab - 1
         )
 
-    chunk = 4 * LANES
+    def groups_of(k):
+        return (width * k) // LANES, -(-(width * (rows - 1 - k)) // LANES)
+
     kpad = cw.shape[0]
     per_group = LANES // kpad
     lane = lax.broadcasted_iota(jnp.int32, (8, LANES), 1)
@@ -274,13 +276,16 @@
     def build(c):
         w6[...] = dense[c].astype(jnp.bfloat16)
 
-        @pl.loop(0, cells // chunk)
-        def _(n):
-            at = pl.ds(pl.multiple_of(n * chunk, chunk), chunk)
+        first, last = groups_of(c)
+        for start in range(first, last, 4):
+            stop = min(start + 4, last)
             for table, a6 in ((ax, a6x), (ay, a6y)):
-                got = jnp.dot(w6[...], a6[:, at], preferred_element_type=jnp.float32)
-                for q in range(chunk // LANES):
-                    table[c, n * (chunk // LANES) + q] = got[:, q * LANES : (q + 1) * LANES]
+                got = jnp.dot(
+                    w6[...], a6[:, start * LANES : stop * LANES],
+                    preferred_element_type=jnp.float32,
+                )
+                for q in range(stop - start):
+                    table[c, start + q] = got[:, q * LANES : (q + 1) * LANES]
 
     build(0)
     for d in range(owners):
@@ -318,21 +323,23 @@
 
     for k in range(steps):
         c = k % batches
-        pieces = []
+        first, last = groups_of(k)
+        reach = -(-(width * (rows - k)) // LANES)
+        size = (reach - first) * LANES
+        span = pl.ds(first * LANES, size)
+        scale = inv[:, span]
+        row = lax.broadcasted_iota(jnp.int32, (mode_dev, size), 0)
+        active = (row >= c * per_batch) & (row < (c + 1) * per_batch)
         for o in range(owners):
-            mine = pl.ds(o * mode_dev + c * per_batch, per_batch)
-            u = r[mine, :] * inv[...]
-            sol[mine, :] = sol[mine, :] + u
-            pieces.append(u)
-        u = jnp.concatenate(pieces, axis=0)
-        dvx[...] = u - pltpu.roll(u, cells - width, 1)
-        dvy[...] = u - pltpu.roll(u, cells - 1, 1)
+            mine = pl.ds(o * mode_dev, mode_dev)
+            u = r[mine, span] * scale
+            dvx[mine, span] = u - pltpu.roll(u, size - width, 1)
+            dvy[mine, span] = u - pltpu.roll(u, size - 1, 1)
+            sol[mine, span] = sol[mine, span] + jnp.where(active, u, 0.0)
         if k == steps - 1:
             pack(0, sol)
             for d in range(1, owners):
                 out_copy(0, d).start()
-        first = (width * k) // LANES
-        last = -(-(width * (rows - 1 - k)) // LANES)
 
         @pl.loop(first, last)
         def _(g):
@@ -340,7 +347,8 @@
             for table, diff, out in ((ax, dvx, ex), (ay, dvy, ey)):
                 sums = [None] * blocks
                 for s in range(sources):
-                    dv = jnp.broadcast_to(diff[pl.ds(s, 1), at], (8, LANES))
+                    line = (s // per_batch) * mode_dev + c * per_batch + s % per_batch
+                    dv = jnp.broadcast_to(diff[pl.ds(line, 1), at], (8, LANES))
                     for b in range(blocks):
                         term = table[c, g, pl.ds(s * modes + b * 8, 8), :] * dv
                         sums[b] = term if s == 0 else sums[b] + term
@@ -447,7 +455,6 @@
     vmem = pl.BlockSpec(memory_space=pltpu.VMEM)
     table = pltpu.VMEM((batches, cells // LANES, sources * modes, LANES), jnp.float32)
     state = pltpu.VMEM((modes, cells), jnp.float32)
-    diff = pltpu.VMEM((sources, cells), jnp.float32)
     coef6 = pltpu.VMEM((8 * kpad, cells), jnp.bfloat16)
     back = pl.pallas_call(
         functools.partial(sweep_kernel, dims),
@@ -461,8 +468,8 @@
             state,
             state,
             state,
-            diff,
-            diff,
+            state,
+            state,
             pltpu.VMEM((sources * modes, 8 * kpad), jnp.bfloat16),
             coef6,
             coef6,

time: 54.3 us -> 53 us (0.976)
  Pallas kernels: 41.2 us -> 39.9 us
    pallas_call x1, Pallas kernels: 41.2 us -> 39.9 us  [by_patch(): pl.pallas_call(functools.partial(sweep_kernel, dims), out_shape=jax.Shape...]
where the time goes in v5:
time: 53 us; the launch traced here: 52.5 us
  Pallas kernels  39.9 us (75%)
  local copies, waits for them, and re-layouts  10 us (19%)
  other arithmetic  1.66 us (3%)
  between operations  0.9 us (2%)
    pallas_call x1, Pallas kernels, by_patch(): pl.pallas_call(functools.partial(sweep_kernel, dims), out_shape=jax.Shape...  39.9 us
    unnamed x26, local copies, waits for them, and re-layouts  3.17 us
    reshape x2, local copies, waits for them, and re-layouts, by_patch(): back = back.reshape(2, owners, mode_dev, slab, cols)  1.83 us
    broadcast_in_dim x18, local copies, waits for them, and re-layouts, reorder(): jnp.where(table[:, j].reshape((-1,) + (1,) * (x.ndim - 1)), x[j][None], j...  1.44 us

profile of v5, /device:TPU:0, one launch (start us, length us, event | category | flops | bytes accessed | tf_op | source)
XLA Modules:
  0.0 52.5 jit_solution(17352912170834713031)
XLA Ops:
  0.7 0.6 %copy-done.7 = s32[64]{0:T(128)S(1)} copy-done((s32[64]{0:T(128)S(1)}, s32[64]{0:T(128)}, u32[]{:S(2)}) %copy-start.7) | copy-done | bytes 280
  1.3 0.1 eq.51
  1.4 0.3 convert_reduce_fusion
  1.7 0.1 reshape.99
  1.8 0.1 dynamic_slice.6
  1.8 0.1 iota_compare_fusion.3
  1.9 0.7 %copy-done.5 = s32[4,8,24]{2,1,0:T(8,128)S(1)} copy-done((s32[4,8,24]{2,1,0:T(8,128)S(1)}, s32[4,8,24]{2,1,0:T(8,128)}, u32[]{:S(2)}) %copy-start.5) | copy-done | bytes 3096
  2.7 0.7 %select_reduce_fusion = s32[4,8,24]{2,1,0:T(8,128)S(1)} fusion(s32[64]{0:T(128)S(1)} %get-tuple-element.56, s32[4,8,24]{2,1,0:T(8,128)S(1)} %copy-done.5), kind=kLoop, calls=%fused_computation.2 | loop fusion | flops 146688 | bytes 6400 | tf_op jit(solution)/shard_map/reduce_sum | solution.py:421
  3.4 0.7 %copy-done.6 = f32[4,8,24]{2,1,0:T(8,128)S(1)} copy-done((f32[4,8,24]{2,1,0:T(8,128)S(1)}, f32[4,8,24]{2,1,0:T(8,128)}, u32[]{:S(2)}) %copy-start.6) | copy-done | bytes 3096
  4.1 0.1 slice_reduce_fusion.7
  4.3 0.1 broadcast_in_dim.424
  4.3 0.1 broadcast_in_dim.446
  4.4 0.1 broadcast_in_dim.443
  4.5 0.1 broadcast_in_dim.440
  4.6 0.1 broadcast_in_dim.437
  4.7 0.1 broadcast_in_dim.434
  4.8 0.1 broadcast_in_dim.431
  4.8 0.1 broadcast_in_dim.428
  4.9 0.1 select_add_fusion.2
  5.0 0.6 %pad_bitcast_fusion.pairs = f32[8,256]{1,0:T(8,128)} fusion(f32[8,2,96]{2,0,1:T(8,128)S(1)} %select_add_fusion.2), kind=kLoop, calls=%fused_computation.39 | loop fusion | bytes 14336 | tf_op jit(solution)/shard_map/reshape | solution.py:444
  5.7 0.1 select_add_fusion.1
  5.8 0.2 pad_slice_fusion
  6.0 0.1 stack.55
  6.1 0.1 stack.54
  6.2 0.1 stack.53
  6.3 0.1 stack.52
  6.4 0.1 stack.51
  6.5 0.1 stack.50
  6.6 0.1 stack.49
  6.7 0.1 stack.48
  6.9 0.4 copy-done
  7.3 0.6 %copy-done.2 = f32[8,8,768]{2,1,0:T(8,128)} copy-done((f32[8,8,768]{2,1,0:T(8,128)}, f32[8,8,768]{2,1,0:T(8,128)S(1)}, u32[]{:S(2)}) %copy-start.2) | copy-done | bytes 196632
  7.9 0.1 constant_dynamic-update-slice_fusion.11
  8.0 0.1 pad_dynamic-slice_fusion
  8.2 0.8 %reshape.101.cw = f32[32,768]{1,0:T(8,128)} reshape(f32[32,16,48]{2,1,0:T(8,128)S(1)} %pad_dynamic-slice_fusion) | data formatting | bytes 196608 | tf_op jit(solution)/shard_map/reshape | solution.py:453
  9.0 39.9 %sweeps.1 = f32[2,8,8,512]{3,2,1,0:T(8,128)} custom-call(f32[8,8,768]{2,1,0:T(8,128)} %copy-done.2, f32[8,256]{1,0:T(8,128)} %pad_bitcast_fusion.pairs, f32[32,768]{1,0:T(8,128)} %reshape.101.cw), custom_call_target="tpu_custom_call" | custom-call | tf_op jit(solution)/shard_map/sweeps/pallas_call | solution.py:459
  48.9 1.2 %reshape.102 = f32[2,8,8,16,32]{4,3,2,1,0:T(8,128)S(1)} reshape(f32[2,8,8,512]{3,2,1,0:T(8,128)} %sweeps.1) | data formatting | bytes 524288 | tf_op jit(solution)/shard_map/reshape | solution.py:494
  50.1 0.6 %copy.12 = f32[2,8,8,16,32]{4,1,3,0,2:T(8,128)S(1)} copy(f32[2,8,8,16,32]{4,3,2,1,0:T(8,128)S(1)} %reshape.102) | data formatting | bytes 524288 | tf_op jit(solution)/shard_map/reshape | solution.py:494
  50.8 0.1 broadcast_in_dim.448
  50.9 0.1 broadcast_in_dim.477
  51.0 0.1 broadcast_in_dim.473
  51.1 0.1 broadcast_in_dim.469
  51.2 0.1 broadcast_in_dim.465
  51.3 0.1 broadcast_in_dim.461
  51.4 0.1 broadcast_in_dim.457
  51.5 0.1 broadcast_in_dim.453
  51.6 0.2 select_add_fusion
  51.8 0.7 %slice_bitcast_fusion = (f32[8,16,256]{2,1,0:T(8,128)}, f32[8,16,256]{2,1,0:T(8,128)}) fusion(f32[8,2,16,256]{3,2,0,1:T(8,128)S(1)} %select_add_fusion), kind=kLoop, calls=%fused_computation.7 | loop fusion | bytes 524288 | tf_op jit(solution)/shard_map/squeeze | solution.py:497
  (31 shorter events, 0.3 us)
Async XLA Ops:
  0.6 0.7 %copy-start.7 = (s32[64]{0:T(128)S(1)}, s32[64]{0:T(128)}, u32[]{:S(2)}) copy-start(s32[64]{0:T(128)} %param.10) | copy-start | bytes 772
  1.9 0.7 %copy-start.5 = (s32[4,8,24]{2,1,0:T(8,128)S(1)}, s32[4,8,24]{2,1,0:T(8,128)}, u32[]{:S(2)}) copy-start(s32[4,8,24]{2,1,0:T(8,128)} %param.11) | copy-start | bytes 9220
  2.6 0.8 %copy-start.4 = (s32[4,8,24]{2,1,0:T(8,128)S(1)}, s32[4,8,24]{2,1,0:T(8,128)}, u32[]{:S(2)}) copy-start(s32[4,8,24]{2,1,0:T(8,128)} %param.12) | copy-start | bytes 9220
  3.4 0.7 %copy-start.6 = (f32[4,8,24]{2,1,0:T(8,128)S(1)}, f32[4,8,24]{2,1,0:T(8,128)}, u32[]{:S(2)}) copy-start(f32[4,8,24]{2,1,0:T(8,128)} %param.13) | copy-start | bytes 9220
  4.1 1.5 %copy-start.3 = (f32[8,16,256]{2,1,0:T(8,128)S(1)}, f32[8,16,256]{2,1,0:T(8,128)}, u32[]{:S(2)}) copy-start(f32[8,16,256]{2,1,0:T(8,128)} %param.7) | copy-start | bytes 393220
  4.9 0.7 %copy-start.1 = (f32[16,256]{1,0:T(8,128)S(1)}, f32[16,256]{1,0:T(8,128)}, u32[]{:S(2)}) copy-start(f32[16,256]{1,0:T(8,128)} %param.8) | copy-start | bytes 49156
  6.2 1.0 %copy-start = (f32[28,16,256]{2,1,0:T(8,128)S(1)}, f32[28,16,256]{2,1,0:T(8,128)}, u32[]{:S(2)}) copy-start(f32[28,16,256]{2,1,0:T(8,128)} %param.9) | copy-start | bytes 1376260
  7.2 0.7 %copy-start.2 = (f32[8,8,768]{2,1,0:T(8,128)}, f32[8,8,768]{2,1,0:T(8,128)S(1)}, u32[]{:S(2)}) copy-start(f32[8,8,768]{2,1,0:T(8,128)S(1)} %constant_dynamic-update-slice_fusion.win) | copy-start | bytes 589828

commit v6 on v5

--- a/solution.py
+++ b/solution.py
@@ -341,8 +341,7 @@
             for d in range(1, owners):
                 out_copy(0, d).start()
 
-        @pl.loop(first, last)
-        def _(g):
+        def accumulate(g):
             at = pl.ds(pl.multiple_of(g * LANES, LANES), LANES)
             for table, diff, out in ((ax, dvx, ex), (ay, dvy, ey)):
                 sums = [None] * blocks
@@ -354,6 +353,14 @@
                         sums[b] = term if s == 0 else sums[b] + term
                 for b in range(blocks):
                     out[pl.ds(b * 8, 8), at] = sums[b]
+
+        @pl.loop(0, (last - first) // 2)
+        def _(n):
+            accumulate(first + 2 * n)
+            accumulate(first + 2 * n + 1)
+
+        if (last - first) % 2:
+            accumulate(last - 1)
 
         for b in range(blocks):
             some = pl.ds(b * 8, 8)

time: 53 us -> 52.5 us (level)
  no operation moved by 1% of the time
where the time goes in v6:
time: 52.5 us; the launch traced here: 52 us
  Pallas kernels  39.4 us (75%)
  local copies, waits for them, and re-layouts  10 us (19%)
  other arithmetic  1.66 us (3%)
  between operations  0.9 us (2%)
    pallas_call x1, Pallas kernels, by_patch(): pl.pallas_call(functools.partial(sweep_kernel, dims), out_shape=jax.Shape...  39.4 us
    unnamed x26, local copies, waits for them, and re-layouts  3.17 us
    reshape x2, local copies, waits for them, and re-layouts, by_patch(): back = back.reshape(2, owners, mode_dev, slab, cols)  1.83 us
    broadcast_in_dim x18, local copies, waits for them, and re-layouts, reorder(): jnp.where(table[:, j].reshape((-1,) + (1,) * (x.ndim - 1)), x[j][None], j...  1.44 us

profile of v6, /device:TPU:0, one launch (start us, length us, event | category | flops | bytes accessed | tf_op | source)
XLA Modules:
  0.0 52.0 jit_solution(1916206149822056744)
XLA Ops:
  0.7 0.6 %copy-done.7 = s32[64]{0:T(128)S(1)} copy-done((s32[64]{0:T(128)S(1)}, s32[64]{0:T(128)}, u32[]{:S(2)}) %copy-start.7) | copy-done | bytes 280
  1.3 0.1 eq.51
  1.4 0.3 convert_reduce_fusion
  1.7 0.1 reshape.99
  1.8 0.1 dynamic_slice.6
  1.8 0.1 iota_compare_fusion.3
  1.9 0.7 %copy-done.5 = s32[4,8,24]{2,1,0:T(8,128)S(1)} copy-done((s32[4,8,24]{2,1,0:T(8,128)S(1)}, s32[4,8,24]{2,1,0:T(8,128)}, u32[]{:S(2)}) %copy-start.5) | copy-done | bytes 3096
  2.7 0.7 %select_reduce_fusion = s32[4,8,24]{2,1,0:T(8,128)S(1)} fusion(s32[64]{0:T(128)S(1)} %get-tuple-element.56, s32[4,8,24]{2,1,0:T(8,128)S(1)} %copy-done.5), kind=kLoop, calls=%fused_computation.2 | loop fusion | flops 146688 | bytes 6400 | tf_op jit(solution)/shard_map/reduce_sum | solution.py:428
  3.4 0.7 %copy-done.6 = f32[4,8,24]{2,1,0:T(8,128)S(1)} copy-done((f32[4,8,24]{2,1,0:T(8,128)S(1)}, f32[4,8,24]{2,1,0:T(8,128)}, u32[]{:S(2)}) %copy-start.6) | copy-done | bytes 3096
  4.1 0.1 slice_reduce_fusion.7
  4.3 0.1 broadcast_in_dim.424
  4.3 0.1 broadcast_in_dim.446
  4.4 0.1 broadcast_in_dim.443
  4.5 0.1 broadcast_in_dim.440
  4.6 0.1 broadcast_in_dim.437
  4.7 0.1 broadcast_in_dim.434
  4.8 0.1 broadcast_in_dim.431
  4.8 0.1 broadcast_in_dim.428
  4.9 0.1 select_add_fusion.2
  5.0 0.6 %pad_bitcast_fusion.pairs = f32[8,256]{1,0:T(8,128)} fusion(f32[8,2,96]{2,0,1:T(8,128)S(1)} %select_add_fusion.2), kind=kLoop, calls=%fused_computation.39 | loop fusion | bytes 14336 | tf_op jit(solution)/shard_map/reshape | solution.py:451
  5.7 0.1 select_add_fusion.1
  5.8 0.2 pad_slice_fusion
  6.0 0.1 stack.55
  6.1 0.1 stack.54
  6.2 0.1 stack.53
  6.3 0.1 stack.52
  6.4 0.1 stack.51
  6.5 0.1 stack.50
  6.6 0.1 stack.49
  6.7 0.1 stack.48
  6.9 0.4 copy-done
  7.3 0.6 %copy-done.2 = f32[8,8,768]{2,1,0:T(8,128)} copy-done((f32[8,8,768]{2,1,0:T(8,128)}, f32[8,8,768]{2,1,0:T(8,128)S(1)}, u32[]{:S(2)}) %copy-start.2) | copy-done | bytes 196632
  7.9 0.1 constant_dynamic-update-slice_fusion.11
  8.0 0.1 pad_dynamic-slice_fusion
  8.2 0.8 %reshape.101.cw = f32[32,768]{1,0:T(8,128)} reshape(f32[32,16,48]{2,1,0:T(8,128)S(1)} %pad_dynamic-slice_fusion) | data formatting | bytes 196608 | tf_op jit(solution)/shard_map/reshape | solution.py:460
  9.0 39.4 %sweeps.1 = f32[2,8,8,512]{3,2,1,0:T(8,128)} custom-call(f32[8,8,768]{2,1,0:T(8,128)} %copy-done.2, f32[8,256]{1,0:T(8,128)} %pad_bitcast_fusion.pairs, f32[32,768]{1,0:T(8,128)} %reshape.101.cw), custom_call_target="tpu_custom_call" | custom-call | tf_op jit(solution)/shard_map/sweeps/pallas_call | solution.py:466
  48.4 1.2 %reshape.102 = f32[2,8,8,16,32]{4,3,2,1,0:T(8,128)S(1)} reshape(f32[2,8,8,512]{3,2,1,0:T(8,128)} %sweeps.1) | data formatting | bytes 524288 | tf_op jit(solution)/shard_map/reshape | solution.py:501
  49.6 0.6 %copy.12 = f32[2,8,8,16,32]{4,1,3,0,2:T(8,128)S(1)} copy(f32[2,8,8,16,32]{4,3,2,1,0:T(8,128)S(1)} %reshape.102) | data formatting | bytes 524288 | tf_op jit(solution)/shard_map/reshape | solution.py:501
  50.3 0.1 broadcast_in_dim.448
  50.4 0.1 broadcast_in_dim.477
  50.5 0.1 broadcast_in_dim.473
  50.6 0.1 broadcast_in_dim.469
  50.7 0.1 broadcast_in_dim.465
  50.8 0.1 broadcast_in_dim.461
  50.9 0.1 broadcast_in_dim.457
  51.0 0.1 broadcast_in_dim.453
  51.1 0.2 select_add_fusion
  51.3 0.7 %slice_bitcast_fusion = (f32[8,16,256]{2,1,0:T(8,128)}, f32[8,16,256]{2,1,0:T(8,128)}) fusion(f32[8,2,16,256]{3,2,0,1:T(8,128)S(1)} %select_add_fusion), kind=kLoop, calls=%fused_computation.7 | loop fusion | bytes 524288 | tf_op jit(solution)/shard_map/squeeze | solution.py:504
  (31 shorter events, 0.3 us)
Async XLA Ops:
  0.6 0.7 %copy-start.7 = (s32[64]{0:T(128)S(1)}, s32[64]{0:T(128)}, u32[]{:S(2)}) copy-start(s32[64]{0:T(128)} %param.10) | copy-start | bytes 772
  1.9 0.7 %copy-start.5 = (s32[4,8,24]{2,1,0:T(8,128)S(1)}, s32[4,8,24]{2,1,0:T(8,128)}, u32[]{:S(2)}) copy-start(s32[4,8,24]{2,1,0:T(8,128)} %param.11) | copy-start | bytes 9220
  2.6 0.8 %copy-start.4 = (s32[4,8,24]{2,1,0:T(8,128)S(1)}, s32[4,8,24]{2,1,0:T(8,128)}, u32[]{:S(2)}) copy-start(s32[4,8,24]{2,1,0:T(8,128)} %param.12) | copy-start | bytes 9220
  3.4 0.7 %copy-start.6 = (f32[4,8,24]{2,1,0:T(8,128)S(1)}, f32[4,8,24]{2,1,0:T(8,128)}, u32[]{:S(2)}) copy-start(f32[4,8,24]{2,1,0:T(8,128)} %param.13) | copy-start | bytes 9220
  4.1 1.5 %copy-start.3 = (f32[8,16,256]{2,1,0:T(8,128)S(1)}, f32[8,16,256]{2,1,0:T(8,128)}, u32[]{:S(2)}) copy-start(f32[8,16,256]{2,1,0:T(8,128)} %param.7) | copy-start | bytes 393220
  4.9 0.7 %copy-start.1 = (f32[16,256]{1,0:T(8,128)S(1)}, f32[16,256]{1,0:T(8,128)}, u32[]{:S(2)}) copy-start(f32[16,256]{1,0:T(8,128)} %param.8) | copy-start | bytes 49156
  6.2 1.0 %copy-start = (f32[28,16,256]{2,1,0:T(8,128)S(1)}, f32[28,16,256]{2,1,0:T(8,128)}, u32[]{:S(2)}) copy-start(f32[28,16,256]{2,1,0:T(8,128)} %param.9) | copy-start | bytes 1376260
  7.2 0.7 %copy-start.2 = (f32[8,8,768]{2,1,0:T(8,128)}, f32[8,8,768]{2,1,0:T(8,128)S(1)}, u32[]{:S(2)}) copy-start(f32[8,8,768]{2,1,0:T(8,128)S(1)} %constant_dynamic-update-slice_fusion.win) | copy-start | bytes 589828
